TPU v7x, 256 devices: a whole 4x4x8 slice. The times are simulated.
256 devices in a mesh: contacts: 32 (over y, z), tm: 8 (over x, core).
Axes of the slice: x: 4, y: 4, z: 8, core: 2. Of those that a mesh axis runs over, the one named last changes fastest.
Arguments:
- signal: bfloat16 [8192, 1024], P('contacts', 'tm'), may hold values from -6 to 6
- pos_idx: int32 [8192], P('contacts'), may hold values from 0 to 4095
- live_count: int32 [32], P('contacts'), may hold values from 128 to 256, as said below
- latents: bfloat16 [256, 512], replicated, may hold values from -400 to 400
- pos_table: bfloat16 [4096, 512], replicated, may hold values from -6 to 6
- w_in: bfloat16 [32, 512], replicated, may hold values from -1 to 1
- w_kv: bfloat16 [512, 1024], replicated, may hold values from -0.25 to 0.25
- w_query: bfloat16 [512, 512], replicated, may hold values from -0.25 to 0.25
- w_out: bfloat16 [512, 512], replicated, may hold values from -0.25 to 0.25
- conv_weight: bfloat16 [2, 3, 512, 512], replicated, may hold values from -0.15625 to 0.15625
- conv_bias: float32 [2, 512], replicated, may hold values from -3 to 3
- cotangent: bfloat16 [32, 256, 512], P('tm', 'contacts'), may hold values from -6 to 6
Outputs:
- features: bfloat16 [32, 256, 512], P('tm', 'contacts')
- d_latents: float32 [256, 512], replicated
Inputs may be any that keep to these rules, and one draw needn't show every extreme that they name: The first live_count[b] contacts of block b are valid; some block is full and some block has exactly 128 valid contacts.
All inputs are finite; a program needn't handle non-finite values.
Results may differ from a plain program's by a relative error of at most 0.018.
The roundings to bfloat16 on the way count: a program that leaves them out, or rounds other values in their place, can miss the bound.
Values may be sent and summed in bfloat16 or wider, within the bound.
No kernel may reach another device: no remote copies, remote signals or barrier semaphores. Data moves between devices by JAX's collectives and lax.ppermute only.
A program may use at most 192 MiB of HBM per device.

v0:
```python
import functools

import jax
import jax.numpy as jnp
from jax import lax
from jax.experimental import pallas as pl
from jax.experimental.pallas import tpu as pltpu
from jax.sharding import Mesh
from jax.sharding import PartitionSpec as P

HD = 64
PATCH = 32
KSIZE = 3
LAYERS = 2

neg_big = -1e30
scale_dot = 0.125

bf16 = jnp.bfloat16
f32 = jnp.float32

NY, NZ, NTM = 4, 8, 8
MIB = 1 << 20
PIECE, PARTS, HALVES, VMEM_ABSORB = 2048, 2, 2, 28
WUNROLL, VMEM_BACK = 4, 40


def nt_dot(a, b):
    return lax.dot_general(a, b, (((1,), (1,)), ((), ())), preferred_element_type=f32)


def nn_dot(a, b):
    return jnp.dot(a, b, preferred_element_type=f32)


def head_of_lane(shape):
    return lax.broadcasted_iota(jnp.int32, shape, len(shape) - 1) // HD


def spread_heads(rows, heads):
    head = head_of_lane(rows.shape)
    zero = jnp.zeros_like(rows)
    return jnp.concatenate([jnp.where(head == h, rows, zero) for h in range(heads)], axis=0)


def collect_heads(blocks, heads):
    r = blocks.shape[0] // heads
    head = head_of_lane((r, blocks.shape[1]))
    out = blocks[:r]
    for h in range(1, heads):
        out = jnp.where(head == h, blocks[h * r : (h + 1) * r], out)
    return out


def columns_to_lanes(column, heads, first, base):
    r = base.shape[0]
    lane = lax.broadcasted_iota(jnp.int32, base.shape, 1)
    for h in range(heads):
        base = jnp.where(lane == first + h, column[h * r : (h + 1) * r], base)
    return base


def lanes_to_column(stats, heads, first):
    return jnp.concatenate([stats[:, first + h : first + h + 1] for h in range(heads)], axis=0)


def lanes_to_columns_wide(stats, heads, first):
    r = stats.shape[0]
    head = head_of_lane((r, heads * HD))
    out = jnp.broadcast_to(stats[:, first : first + 1], (r, heads * HD))
    for h in range(1, heads):
        out = jnp.where(head == h, stats[:, first + h : first + h + 1], out)
    return out


def silu_slope(pre_act):
    sigmoid_v = jax.nn.sigmoid(pre_act)
    return sigmoid_v * (1.0 + pre_act * (1.0 - sigmoid_v))


def rounded(value):
    return value.astype(bf16).astype(f32)


def absorb_kernel(*refs, fresh, last, count):
    refs = list(refs)
    messages = [refs.pop(0) for _ in range(count)]
    q_ref, w_in_ref, w_kv_ref, table_ref = (refs.pop(0) for _ in range(4))
    if not fresh:
        acc_in, stat_in = refs.pop(0), refs.pop(0)
    kv_hbm, valid_ref = refs.pop(0), refs.pop(0)
    if last:
        part_refs = [refs.pop(0) for _ in range(NY)]
    else:
        acc_out, stat_out = refs.pop(0), refs.pop(0)
    pos_ref, tok_ref, kv_ref, sem = refs
    width = q_ref.shape[1]
    heads = width // HD
    con_dev, span = messages[0].shape[0], messages[0].shape[1] - 128
    windows = span // PATCH
    rows = count * con_dev
    message = jnp.concatenate([m[...] for m in messages], axis=0)
    sig = message[:, :span]
    meta = message[:, span:].astype(f32)
    idx = meta[:, 0:1] * 64.0 + meta[:, 1:2]
    lane = lax.broadcasted_iota(jnp.int32, (1, con_dev), 1).astype(f32)
    valid = jnp.concatenate(
        [jnp.where(lane < meta[c * con_dev : c * con_dev + 1, 2:3], 1.0, 0.0) for c in range(count)], axis=1
    )
    valid_ref[...] = jnp.broadcast_to(valid, valid_ref.shape)
    piece = PIECE
    ids = lax.broadcasted_iota(jnp.int32, (rows, piece), 1).astype(f32)
    pos_ref[...] = jnp.zeros_like(pos_ref)

    @pl.loop(0, table_ref.shape[0] // piece)
    def _(k):
        start = pl.multiple_of(k * piece, piece)
        hot = jnp.where(ids == idx - start.astype(f32), 1.0, 0.0).astype(bf16)
        pos_ref[...] = pos_ref[...] + nn_dot(hot, table_ref[pl.ds(start, piece), :])

    tall = jnp.concatenate([w_in_ref[...]] * windows, axis=0)
    band = lax.broadcasted_iota(jnp.int32, sig.shape, 1) // PATCH
    for w in range(windows):
        embedded = nn_dot(jnp.where(band == w, sig, jnp.zeros_like(sig)), tall)
        tok_ref[w * rows : (w + 1) * rows, :] = (embedded + pos_ref[...]).astype(bf16)
    ws = windows // PARTS

    def send(part):
        here = pl.ds(part * ws, ws)
        return pltpu.make_async_copy(kv_ref.at[here], kv_hbm.at[here], sem.at[part])

    def project(part):
        tokens = tok_ref[pl.ds(pl.multiple_of(part * ws * rows, ws * rows), ws * rows), :]
        for half in range(HALVES):
            cols = slice(half * 2 * width // HALVES, (half + 1) * 2 * width // HALVES)
            keyval = nn_dot(tokens, w_kv_ref[:, cols]).astype(bf16)
            kv_ref[pl.ds(part * ws, ws), :, cols] = keyval.reshape(ws, rows, 2 * width // HALVES)
        send(part).start()

    if count == 1:
        for part in range(PARTS):
            project(part)
    else:
        pl.loop(0, PARTS)(project)
    q_wide = spread_heads(q_ref[...], heads)

    def one_window(w):
        scores = nt_dot(q_wide, kv_ref[w, :, :width]) * scale_dot
        scores = jnp.where(valid > 0.0, scores, neg_big)
        top = jnp.max(scores, axis=1, keepdims=True)
        if not fresh:
            before, total_before = stat_in[w, :, 0:1], stat_in[w, :, 1:2]
            top = jnp.maximum(top, before)
        weights = jnp.exp(scores - top)
        totals = jnp.sum(weights, axis=1, keepdims=True)
        accum = nn_dot(weights.astype(bf16), kv_ref[w, :, width:])
        if not fresh:
            fade = jnp.exp(before - top)
            totals = totals + total_before * fade
            accum = accum + acc_in[w] * fade
        if not last:
            acc_out[w] = accum
            stat_out[w, :, 0:1] = top
            stat_out[w, :, 1:2] = totals
        else:
            mixed = collect_heads(accum, heads)
            stats = jnp.zeros((mixed.shape[0], 128), f32)
            stats = columns_to_lanes(top, heads, 0, stats)
            stats = columns_to_lanes(totals, heads, heads, stats)
            each = mixed.shape[0] // NY
            for s, part_ref in enumerate(part_refs):
                part_ref[w, :, :width] = mixed[s * each : (s + 1) * each]
                part_ref[w, :, width:] = stats[s * each : (s + 1) * each]

    together = WUNROLL // count

    @pl.loop(0, windows // together)
    def _(k):
        for part in range(together):
            one_window(k * together + part)

    for part in range(PARTS):
        send(part).wait()


def absorb(messages, q, w_in, w_kv, table, state, last):
    count = len(messages)
    lat, width = q.shape
    con_dev = messages[0].shape[0]
    windows = (messages[0].shape[1] - 128) // PATCH
    rows = lat * (width // HD)
    fresh = state is None
    vmem = pl.BlockSpec(memory_space=pltpu.VMEM)
    operands = list(messages) + [q, w_in, w_kv, table]
    in_specs = [vmem] * len(operands)
    aliases = {}
    if not fresh:
        n = len(operands)
        operands += list(state)
        in_specs += [vmem, vmem]
        aliases = {} if last else {n: 2, n + 1: 3}
    acc = jax.ShapeDtypeStruct((windows, rows, width), f32)
    stat = jax.ShapeDtypeStruct((windows, rows, 128), f32)
    part = jax.ShapeDtypeStruct((windows, lat // NY, width + 128), f32)
    tail = [part] * NY if last else [acc, stat]
    return pl.pallas_call(
        functools.partial(absorb_kernel, fresh=fresh, last=last, count=count),
        in_specs=in_specs,
        out_specs=[pl.BlockSpec(memory_space=pltpu.HBM)] + [vmem] * (1 + len(tail)),
        out_shape=[
            pltpu.HBM((windows, count * con_dev, 2 * width), bf16),
            jax.ShapeDtypeStruct((8, count * con_dev), f32),
        ]
        + tail,
        scratch_shapes=[
            pltpu.VMEM((count * con_dev, width), f32),
            pltpu.VMEM((windows * count * con_dev, width), bf16),
            pltpu.VMEM((windows, count * con_dev, 2 * width), bf16),
            pltpu.SemaphoreType.DMA((PARTS,)),
        ],
        input_output_aliases=aliases,
        compiler_params=pltpu.CompilerParams(vmem_limit_bytes=VMEM_ABSORB * MIB),
        name="absorb",
    )(*operands)


def combine_kernel(*refs):
    *part_refs, att_ref, copies_ref, stats_ref = refs
    rows, width = att_ref.shape
    heads = width // HD
    lane = lax.broadcasted_iota(jnp.int32, (rows, 128), 1)
    parts = [ref[...].reshape(rows, width + 128) for ref in part_refs]
    top = parts[0][:, width:]
    for part in parts[1:]:
        top = jnp.maximum(top, part[:, width:])
    totals = jnp.zeros((rows, 128), f32)
    accum = jnp.zeros((rows, width), f32)
    for part in parts:
        factor = jnp.exp(jnp.where(lane < heads, part[:, width:] - top, 0.0))
        totals = totals + factor * pltpu.roll(part[:, width:], 128 - heads, 1)
        accum = accum + part[:, :width] * lanes_to_columns_wide(factor, heads, 0)
    totals = jnp.where(lane < heads, totals, 1.0)
    att = (accum / lanes_to_columns_wide(totals, heads, 0)).astype(bf16)
    att_ref[...] = att
    for t in range(NTM):
        copies_ref[t] = att
    stats_ref[...] = jnp.where(lane < heads, top, pltpu.roll(1.0 / totals, heads, 1))


def combine(parts):
    windows, each, wide = parts[0].shape
    rows = windows * each
    return pl.pallas_call(
        combine_kernel,
        out_shape=[
            jax.ShapeDtypeStruct((rows, wide - 128), bf16),
            jax.ShapeDtypeStruct((NTM, rows, wide - 128), bf16),
            jax.ShapeDtypeStruct((rows, 128), f32),
        ],
        compiler_params=pltpu.CompilerParams(vmem_limit_bytes=8 * MIB),
        name="combine_parts",
    )(*parts)


def conv_kernel(
    tm_ref, own_ref, all_ref, stats_ref, cl_ref, cot_ref, cr_ref,
    w_out_ref, bias_ref, conv_hbm, *refs,
):
    n = (len(refs) - 6) // 2
    kv_hbms, (feat_ref, msg_ref), kv_refs = refs[:n], refs[n : n + 2], refs[n + 2 : 2 * n + 2]
    ext_ref, conv_ref, sem, kv_sem = refs[2 * n + 2 :]
    fetches = [pltpu.make_async_copy(kv_hbms[i].at[0], kv_refs[i], kv_sem.at[i]) for i in range(n)]
    weights = [pltpu.make_async_copy(conv_hbm.at[l], conv_ref.at[l], sem.at[l]) for l in range(LAYERS)]
    for copy in weights:
        copy.start()
    for copy in fetches:
        copy.start()
    rows, width = own_ref.shape
    heads = width // HD
    windows = 4
    each = rows // windows
    reach = 6
    first = tm_ref[0] * windows - reach
    total_windows = NTM * windows

    def inside(lo, count):
        w = lax.broadcasted_iota(jnp.int32, (count * each, width), 0) // each + (first + lo)
        return jnp.logical_and(w >= 0, w < total_windows)

    side = reach * each
    ext_ref[:side, :] = jnp.zeros((side, width), f32)
    ext_ref[side : side + NTM * rows, :] = all_ref[...].astype(f32)
    ext_ref[side + NTM * rows :, :] = jnp.zeros((side, width), f32)
    att = ext_ref[pl.ds(pl.multiple_of(tm_ref[0] * rows, rows), 2 * side + rows), :]
    w_out = w_out_ref[...]
    x0 = rounded(nn_dot(att.astype(bf16), w_out))
    n0 = 14 * each
    weights[0].wait()
    pre0 = bias_ref[0:1, :] + sum(nn_dot(x0[j * each : j * each + n0].astype(bf16), conv_ref[0, j]) for j in range(KSIZE))
    x1 = rounded(x0[each : each + n0] + jax.nn.silu(pre0))
    x1 = jnp.where(inside(1, 14), x1, 0.0)
    n1 = 10 * each
    weights[1].wait()
    pre1 = bias_ref[1:2, :] + sum(nn_dot(x1[2 * j * each : 2 * j * each + n1].astype(bf16), conv_ref[1, j]) for j in range(KSIZE))
    feat_ref[...] = (x1[5 * each : 9 * each] + jax.nn.silu(pre1[3 * each : 7 * each])).astype(bf16)
    g2 = jnp.concatenate([r[...].astype(f32) for r in (cl_ref, cot_ref, cr_ref)], axis=0)
    gpre1 = rounded(g2 * silu_slope(pre1))
    n2 = 6 * each
    g1 = g2[2 * each : 8 * each] + sum(
        nt_dot(gpre1[(4 - 2 * j) * each : (4 - 2 * j) * each + n2].astype(bf16), conv_ref[1, j]) for j in range(KSIZE)
    )
    gpre0 = rounded(g1 * silu_slope(pre0[4 * each : 10 * each]))
    gpre0 = jnp.where(inside(5, 6), gpre0, 0.0)
    g0 = g1[each : 5 * each] + sum(
        nt_dot(gpre0[(2 - j) * each : (2 - j) * each + rows].astype(bf16), conv_ref[0, j]) for j in range(KSIZE)
    )
    grad_att = rounded(nt_dot(g0.astype(bf16), w_out))
    msg_ref[:, :width] = grad_att.astype(bf16)
    product = grad_att * own_ref[...].astype(f32)
    head = head_of_lane((rows, width))
    lane = lax.broadcasted_iota(jnp.int32, (rows, 128), 1)
    stats = stats_ref[...]
    for h in range(heads):
        delta = jnp.sum(jnp.where(head == h, product, 0.0), axis=1, keepdims=True)
        stats = jnp.where(lane == 2 * heads + h, delta, stats)
    stats = jnp.where(lane < 3 * heads, stats, 0.0)
    high = rounded(stats)
    middle = rounded(stats - high)
    low = (stats - high) - middle
    for copy in fetches:
        copy.wait()
    msg_ref[:, width:] = (high + pltpu.roll(middle, 32, 1) + pltpu.roll(low, 64, 1)).astype(bf16)


def conv_stack(tm, own, everyone, stats, cots, w_out, conv_weight, conv_bias, kvs):
    rows, width = own.shape
    cl, cot, cr = cots
    vmem = pl.BlockSpec(memory_space=pltpu.VMEM)
    return pl.pallas_call(
        conv_kernel,
        in_specs=[pl.BlockSpec(memory_space=pltpu.SMEM)]
        + [vmem] * 8
        + [pl.BlockSpec(memory_space=pltpu.HBM)] * (1 + len(kvs)),
        out_specs=[vmem] * (2 + len(kvs)),
        out_shape=[
            jax.ShapeDtypeStruct((rows, width), bf16),
            jax.ShapeDtypeStruct((rows, width + 128), bf16),
        ]
        + [pltpu.VMEM(kv.shape[1:], kv.dtype) for kv in kvs],
        scratch_shapes=[
            pltpu.VMEM(((NTM + 3) * rows, width), f32),
            pltpu.VMEM(conv_weight.shape, conv_weight.dtype),
            pltpu.SemaphoreType.DMA((LAYERS,)),
            pltpu.SemaphoreType.DMA((len(kvs),)),
        ],
        compiler_params=pltpu.CompilerParams(vmem_limit_bytes=20 * MIB),
        name="conv_stack",
    )(tm, own, everyone, stats, cl, cot, cr, w_out, conv_bias, *(pltpu.with_memory_space_constraint(a, pltpu.HBM) for a in (conv_weight, *kvs)))


def backward_kernel(y_ref, q_ref, *refs, slots):
    msg_refs, refs = refs[:slots], refs[slots:]
    n = (len(refs) - 3) // 4
    first_refs, valid_refs, kv_hbms = refs[:n], refs[n : 2 * n], refs[2 * n : 3 * n]
    dq_ref, acc_ref, *kv_refs, sem = refs[3 * n :]
    width = q_ref.shape[1]
    heads = width // HD
    windows = msg_refs[0].shape[0]

    def fetch(window, i):
        return pltpu.make_async_copy(kv_hbms[i].at[window], kv_refs[i].at[window - 1], sem.at[window - 1, i])

    for window in range(1, windows):
        for i in range(n):
            fetch(window, i).start()

    def one_window(window, blocks):
        msg = jnp.concatenate([r[window].astype(f32) for r in msg_refs], axis=0)
        terms = msg[:, width:]
        stats = terms + pltpu.roll(terms, 96, 1) + pltpu.roll(terms, 64, 1)
        top = lanes_to_column(stats, heads, 0)
        inverse = lanes_to_column(stats, heads, heads)
        delta = lanes_to_column(stats, heads, 2 * heads)
        grad_wide = spread_heads(msg[:, :width].astype(bf16), heads)
        q_wide = spread_heads(q_ref[...], heads)
        accum = 0.0
        for block, valid_ref in zip(blocks, valid_refs):
            key_rows = block[:, :width]
            scores = nt_dot(q_wide, key_rows) * scale_dot
            scores = jnp.where(valid_ref[0:1, :] > 0.0, scores, neg_big)
            prob = jnp.exp(scores - top) * inverse
            grad_prob = nt_dot(grad_wide, block[:, width:])
            dscore = (prob * (grad_prob - delta)).astype(bf16)
            accum = accum + nn_dot(dscore, key_rows)
        return accum

    acc_ref[...] = one_window(0, first_refs)

    @pl.loop(1, windows)
    def _(window):
        for i in range(n):
            fetch(window, i).wait()
        acc_ref[...] = acc_ref[...] + one_window(window, [ref.at[window - 1] for ref in kv_refs])

    dq = collect_heads(acc_ref[...], heads) * scale_dot
    each = dq.shape[0] // slots
    for s in range(slots):
        place = pl.multiple_of(((y_ref[0] + (slots - s)) % slots) * each, each)
        dq_ref[pl.ds(place, each), :] = dq[s * each : (s + 1) * each]


def backward_attention(y, kvs, first, valids, q, msgs):
    lat, width = q.shape
    heads = width // HD
    vmem = pl.BlockSpec(memory_space=pltpu.VMEM)
    kvs = [pltpu.with_memory_space_constraint(kv, pltpu.HBM) for kv in kvs]
    return pl.pallas_call(
        functools.partial(backward_kernel, slots=len(msgs)),
        in_specs=[pl.BlockSpec(memory_space=pltpu.SMEM)]
        + [vmem] * (1 + len(msgs) + len(first) + len(valids))
        + [pl.BlockSpec(memory_space=pltpu.HBM)] * len(kvs),
        out_specs=vmem,
        out_shape=jax.ShapeDtypeStruct((lat, width), f32),
        scratch_shapes=[pltpu.VMEM((lat * heads, width), f32)]
        + [pltpu.VMEM((kv.shape[0] - 1,) + kv.shape[1:], kv.dtype) for kv in kvs]
        + [pltpu.SemaphoreType.DMA((kvs[0].shape[0] - 1, len(kvs)))],
        compiler_params=pltpu.CompilerParams(vmem_limit_bytes=VMEM_BACK * MIB),
        name="backward_attention",
    )(y, q, *msgs, *first, *valids, *kvs)


def shift(count, by):
    return [(i, (i + by) % count) for i in range(count)]


def local(
    signal, pos_idx, live_count, latents, pos_table, w_in, w_kv, w_query, w_out,
    conv_weight, conv_bias, cotangent,
):
    con_dev = signal.shape[0]
    pat_dev = signal.shape[1] // PATCH
    width = w_query.shape[0]
    lat_rows = latents.shape[0]
    y, z, tm = (lax.axis_index(a) for a in ("y", "z", "tm"))
    lat_dev = lat_rows // (NY * NZ)
    up1 = [(i, i + 1) for i in range(NTM - 1)]
    down1 = [(i + 1, i) for i in range(NTM - 1)]

    by_owner = latents.reshape(NY, NZ, lat_dev, width)
    mine = lax.dynamic_index_in_dim(by_owner, z, 1, False)
    slots = jnp.stack([lax.dynamic_index_in_dim(mine, (y + NY - s) % NY, 0, False) for s in range(NY)])
    queries = nn_dot(slots.reshape(NY * lat_dev, width), w_query).astype(bf16)

    lane = lax.broadcasted_iota(jnp.int32, (con_dev, 128), 1)
    index = pos_idx[:, None]
    meta = jnp.where(lane == 0, index // 64, jnp.where(lane == 1, index % 64, live_count[0]))
    own = jnp.concatenate([signal, meta.astype(bf16)], axis=1)

    def absorbed(messages, state, last=False):
        return absorb(messages, queries, w_in, w_kv, pos_table, state, last)

    below, above = own, own
    at_hand, state, kvs, valids = [own], None, [], []
    for step in range(1, NZ // 2 + 1):
        below = lax.ppermute(below, "z", shift(NZ, 1))
        if step < NZ // 2:
            above = lax.ppermute(above, "z", shift(NZ, -1))
        kv, valid, *state = absorbed(at_hand, state)
        kvs.append(kv)
        valids.append(valid)
        if step < NZ // 2:
            below, above, valids[-1] = lax.optimization_barrier((below, above, valids[-1]))
        at_hand = [below, above] if step < NZ // 2 else [below]
    kv, valid, *parts = absorbed(at_hand, state, last=True)
    kvs.append(kv)
    valids.append(valid)

    received = [lax.ppermute(parts[s], "y", shift(NY, -s)) for s in range(1, NY)]

    cot = cotangent.reshape(pat_dev * lat_dev, width)
    cot_late, cot_early, _ = lax.optimization_barrier((cot[lat_dev:], cot[: 3 * lat_dev], parts[0]))
    cot_left = lax.ppermute(cot_late, "tm", up1)
    cot_right = lax.ppermute(cot_early, "tm", down1)

    att, copies, stats = combine([parts[0]] + received)

    everyone = lax.all_to_all(copies, "tm", 0, 0)
    features, msg, *first = conv_stack(
        tm.reshape(1), att, everyone.reshape(-1, width), stats,
        (cot_left, cot, cot_right), w_out, conv_weight, conv_bias, kvs,
    )

    msg = msg.reshape(pat_dev, lat_dev, width + 128)
    msgs = [msg] + [lax.ppermute(msg, "y", shift(NY, s)) for s in range(1, NY)]
    dq = backward_attention(y.reshape(1), kvs, first, valids, queries, msgs)

    pieces = lax.all_to_all(dq, ("y", "tm"), 0, 0, tiled=True)
    dq_row = jnp.sum(pieces, axis=0, keepdims=True).astype(bf16)
    spread = jnp.broadcast_to(dq_row.reshape(1, width // 128, 128), (lat_rows, width // 128, 128))
    dq_all = lax.all_to_all(spread, ("y", "z", "tm"), 0, 0, tiled=True)
    d_latents = nt_dot(dq_all.reshape(lat_rows, width), w_query)
    return features.reshape(pat_dev, lat_dev, width), d_latents


def solution(mesh):
    split = Mesh(mesh.devices.reshape(NY, NZ, NTM), ("y", "z", "tm"))
    contacts = ("y", "z")
    in_specs = (P(contacts, "tm"), P(contacts), P(contacts)) + (P(),) * 8 + (P("tm", contacts, None),)
    out_specs = (P("tm", contacts, None), P())
    return jax.shard_map(local, mesh=split, in_specs=in_specs, out_specs=out_specs, check_vma=False)
```

profile of v0, /device:TPU:1, one launch (start us, length us, event | category | flops | bytes accessed | tf_op | source)
XLA Modules:
  0.0 141.5 jit_solution(12747575170629816262)
XLA Ops:
  0.6 0.0 copy-start
  1.4 0.7 and_select_fusion.1
  2.1 0.1 select_convert_fusion
  2.2 0.9 pad_maximum_fusion.refs_0_
  3.1 6.5 %collective-permute-start.1 = (bf16[256,256]{1,0:T(8,128)(2,1)S(1)}, bf16[256,256]{1,0:T(8,128)(2,1)S(1)}, u32[]{:S(2)}, u32[]{:S(2)}) collective-permute-start(bf16[256,256]{1,0:T(8,128)(2,1)S(1)} %pad_maximum_fusion.refs_0_), channel_id=1, source_target_pairs={{0,56},{8,0},{16,8},{24,16},{32,24},{40,32},{48,40},{56,48},{1,57}... | collective-permute-start | bytes 393224 | tf_op jit(solution)/shard_map/ppermute | solution.py:467
  9.5 0.0 collective-permute-start
  9.5 0.8 dynamic-slice_bitcast_fusion.3
  10.3 0.0 copy-done
  10.3 0.2 convolution_convert_fusion.refs_1_.refs_2_.q_ref
  10.5 0.0 copy-start.1
  10.5 2.2 %copy-done.1 = bf16[4096,512]{1,0:T(8,128)(2,1)S(1)} copy-done((bf16[4096,512]{1,0:T(8,128)(2,1)S(1)}, bf16[4096,512]{1,0:T(8,128)(2,1)}, u32[]{:S(2)}) %copy-start.1) | copy-done | bytes 4194328
  12.7 1.2 copy-done.3
  13.9 0.8 copy-done.4
  14.7 4.1 %absorb.5 = (bf16[4,256,1024]{2,1,0:T(8,128)(2,1)}, f32[8,256]{1,0:T(8,128)S(1)}, f32[4,256,512]{2,1,0:T(8,128)S(1)}, f32[4,256,128]{2,1,0:T(8,128)S(1)}) custom-call(bf16[256,256]{1,0:T(8,128)(2,1)S(1)} %pad_maximum_fusion.refs_0_, bf16[32,512]{1,0:T(8,128)(2,1)S(1)} %convolution_convert_fusion.refs_1_.refs_2_.q_ref, bf16[32,512]{1,0:T(8,128)(2,1)S(1)} %copy-done.4, ...), custom_call_target="tpu_custom_call" | custom-call | tf_op jit(solution)/shard_map/absorb/pallas_call | solution.py:206
  18.8 0.0 collective-permute-done.1.refs_1_
  18.8 0.0 collective-permute-done.refs_0_
  18.8 0.1 collective-permute-start.2
  18.9 2.8 %collective-permute-start.3 = (bf16[256,256]{1,0:T(8,128)(2,1)S(1)}, bf16[256,256]{1,0:T(8,128)(2,1)S(1)}, u32[]{:S(2)}, u32[]{:S(2)}) collective-permute-start(bf16[256,256]{1,0:T(8,128)(2,1)S(1)} %collective-permute-done.1.refs_1_), channel_id=1, source_target_pairs={{0,56},{8,0},{16,8},{24,16},{32,24},{40,32},{48,40},{56,48},{1,57}... | collective-permute-start | bytes 393224 | tf_op jit(solution)/shard_map/ppermute | solution.py:467
  21.6 0.0 copy-done.2
  21.6 8.8 %absorb.6 = (bf16[4,512,1024]{2,1,0:T(8,128)(2,1)}, f32[8,512]{1,0:T(8,128)S(1)}, f32[4,256,512]{2,1,0:T(8,128)S(1)}, f32[4,256,128]{2,1,0:T(8,128)S(1)}) custom-call(bf16[256,256]{1,0:T(8,128)(2,1)S(1)} %collective-permute-done.refs_0_, bf16[256,256]{1,0:T(8,128)(2,1)S(1)} %collective-permute-done.1.refs_1_, ...), custom_call_target="tpu_custom_call", output_to_operand_aliasing={{2}: (6, {}), {3}: (7, {})} | custom-call | tf_op jit(solution)/shard_map/absorb/pallas_call | solution.py:206
  30.5 0.0 collective-permute-done.2.refs_0_
  30.5 0.0 collective-permute-done.3.refs_1_
  30.5 0.1 collective-permute-start.4
  30.6 2.7 %collective-permute-start.5 = (bf16[256,256]{1,0:T(8,128)(2,1)S(1)}, bf16[256,256]{1,0:T(8,128)(2,1)S(1)}, u32[]{:S(2)}, u32[]{:S(2)}) collective-permute-start(bf16[256,256]{1,0:T(8,128)(2,1)S(1)} %collective-permute-done.3.refs_1_), channel_id=1, source_target_pairs={{0,56},{8,0},{16,8},{24,16},{32,24},{40,32},{48,40},{56,48},{1,57}... | collective-permute-start | bytes 393224 | tf_op jit(solution)/shard_map/ppermute | solution.py:467
  33.2 8.8 %absorb.7 = (bf16[4,512,1024]{2,1,0:T(8,128)(2,1)}, f32[8,512]{1,0:T(8,128)S(1)}, f32[4,256,512]{2,1,0:T(8,128)S(1)}, f32[4,256,128]{2,1,0:T(8,128)S(1)}) custom-call(bf16[256,256]{1,0:T(8,128)(2,1)S(1)} %collective-permute-done.2.refs_0_, bf16[256,256]{1,0:T(8,128)(2,1)S(1)} %collective-permute-done.3.refs_1_, ...), custom_call_target="tpu_custom_call", output_to_operand_aliasing={{2}: (6, {}), {3}: (7, {})} | custom-call | tf_op jit(solution)/shard_map/absorb/pallas_call | solution.py:206
  42.1 0.0 collective-permute-done.4.refs_0_
  42.1 0.0 collective-permute-done.5.refs_1_
  42.1 0.1 collective-permute-start.6
  42.2 8.8 %absorb.8 = (bf16[4,512,1024]{2,1,0:T(8,128)(2,1)}, f32[8,512]{1,0:T(8,128)S(1)}, f32[4,256,512]{2,1,0:T(8,128)S(1)}, f32[4,256,128]{2,1,0:T(8,128)S(1)}) custom-call(bf16[256,256]{1,0:T(8,128)(2,1)S(1)} %collective-permute-done.4.refs_0_, bf16[256,256]{1,0:T(8,128)(2,1)S(1)} %collective-permute-done.5.refs_1_, ...), custom_call_target="tpu_custom_call", output_to_operand_aliasing={{2}: (6, {}), {3}: (7, {})} | custom-call | tf_op jit(solution)/shard_map/absorb/pallas_call | solution.py:206
  51.0 0.0 collective-permute-done.6.refs_0_
  51.0 0.0 copy-start.6
  51.0 0.0 copy-start.5
  51.1 0.0 copy-start.7
  51.1 5.6 %absorb.9 = (bf16[4,256,1024]{2,1,0:T(8,128)(2,1)}, f32[8,256]{1,0:T(8,128)S(1)}, f32[4,8,640]{2,1,0:T(8,128)S(1)}, f32[4,8,640]{2,1,0:T(8,128)S(1)}, f32[4,8,64...) custom-call(bf16[256,256]{1,0:T(8,128)(2,1)S(1)} %collective-permute-done.6.refs_0_, ...), custom_call_target="tpu_custom_call" | custom-call | tf_op jit(solution)/shard_map/absorb/pallas_call | solution.py:206
  56.7 2.8 %collective-permute-start.7 = (f32[4,8,640]{2,1,0:T(8,128)S(1)}, f32[4,8,640]{2,1,0:T(8,128)S(1)}, u32[]{:S(2)}, u32[]{:S(2)}) collective-permute-start(f32[4,8,640]{2,1,0:T(8,128)S(1)} %get-tuple-element.63), channel_id=1, source_target_pairs={{0,192},{64,0},{128,64},{192,128},{1,193},{65,1},{129,65},{193,129... | collective-permute-start | bytes 245768 | tf_op jit(solution)/shard_map/ppermute | solution.py:478
  59.5 0.5 collective-permute-start.8
  60.0 0.5 collective-permute-start.9
  60.5 0.4 collective-permute-done.7.refs_1_
  61.0 3.4 %collective-permute-done.8.refs_2_ = f32[4,8,640]{2,1,0:T(8,128)S(1)} collective-permute-done((f32[4,8,640]{2,1,0:T(8,128)S(1)}, f32[4,8,640]{2,1,0:T(8,128)S(1)}, u32[]{:S(2)}, u32[]{:S(2)}) %collective-permute-start.8) | collective-permute-done | bytes 81952 | tf_op jit(solution)/shard_map/ppermute | solution.py:478
  64.3 0.8 collective-permute-done.9.refs_3_
  65.2 1.1 combine_parts.1
  66.3 7.8 %all-to-all-start = ((bf16[8,32,512]{2,1,0:T(8,128)(2,1)}), bf16[8,32,512]{2,1,0:T(8,128)(2,1)S(1)}, u32[]{:S(2)}, u32[]{:S(2)}) async-start(bf16[8,32,512]{2,1,0:T(8,128)(2,1)} %get-tuple-element.67), calls=%async_computation | async-start | bytes 524288 | tf_op jit(solution)/shard_map/all_to_all | solution.py:487
  74.1 0.0 copy-done.6
  74.1 3.5 %collective-permute-start.10 = (bf16[24,512]{1,0:T(8,128)(2,1)S(1)}, bf16[24,512]{1,0:T(8,128)(2,1)S(1)}, u32[]{:S(2)}, u32[]{:S(2)}) collective-permute-start(bf16[24,512]{1,0:T(8,128)(2,1)S(1)} %get-tuple-element.69), channel_id=1, source_target_pairs={{0,1},{1,2},{2,3},{3,4},{4,5},{5,6},{6,7},{8,9},{9,10},{10,11},{11... | collective-permute-start | bytes 73736 | tf_op jit(solution)/shard_map/ppermute | solution.py:482
  77.7 1.9 %collective-permute-start.11 = (bf16[24,512]{1,0:T(8,128)(2,1)S(1)}, bf16[24,512]{1,0:T(8,128)(2,1)S(1)}, u32[]{:S(2)}, u32[]{:S(2)}) collective-permute-start(bf16[24,512]{1,0:T(8,128)(2,1)S(1)} %get-tuple-element.70), channel_id=1, source_target_pairs={{1,0},{2,1},{3,2},{4,3},{5,4},{6,5},{7,6},{9,8},{10,9},{11,10},{12... | collective-permute-start | bytes 73736 | tf_op jit(solution)/shard_map/ppermute | solution.py:483
  79.6 0.0 collective-permute-done.10.cl_ref
  79.6 3.2 %collective-permute-done.11.cr_ref = bf16[24,512]{1,0:T(8,128)(2,1)S(1)} collective-permute-done((bf16[24,512]{1,0:T(8,128)(2,1)S(1)}, bf16[24,512]{1,0:T(8,128)(2,1)S(1)}, u32[]{:S(2)}, u32[]{:S(2)}) %collective-permute-start.11) | collective-permute-done | bytes 24608 | tf_op jit(solution)/shard_map/ppermute | solution.py:483
  82.8 0.0 all-to-all-done
  82.8 0.0 copy-done.5
  82.8 0.0 copy-done.7
  82.8 5.5 %conv_stack.1 = (bf16[32,512]{1,0:T(8,128)(2,1)}, bf16[32,640]{1,0:T(8,128)(2,1)S(1)}, bf16[256,1024]{1,0:T(8,128)(2,1)S(1)}, bf16[512,1024]{1,0:T(8,128)(2,1)S(...) custom-call(s32[1]{0:T(128)} %bitcast.tm_ref, ...), custom_call_target="tpu_custom_call" | custom-call | tf_op jit(solution)/shard_map/conv_stack/pallas_call | solution.py:339
  88.4 0.4 collective-permute-start.14
  88.7 0.7 collective-permute-start.13
  89.4 0.8 collective-permute-start.12
  90.2 1.4 collective-permute-done.14.refs_3_
  91.5 1.6 %collective-permute-done.13.refs_2_ = bf16[4,8,640]{2,1,0:T(8,128)(2,1)S(1)} collective-permute-done((bf16[4,8,640]{2,1,0:T(8,128)(2,1)S(1)}, bf16[4,8,640]{2,1,0:T(8,128)(2,1)S(1)}, u32[]{:S(2)}, u32[]{:S(2)}) %collective-permute-start.13) | collective-permute-done | bytes 40992 | tf_op jit(solution)/shard_map/ppermute | solution.py:494
  93.1 1.0 collective-permute-done.12.refs_1_
  94.1 10.2 %backward_attention.1 = f32[32,512]{1,0:T(8,128)S(1)} custom-call(s32[1]{0:T(128)} %bitcast.13.y_ref, bf16[32,512]{1,0:T(8,128)(2,1)S(1)} %convolution_convert_fusion.refs_1_.refs_2_.q_ref, bf16[4,8,640]{2,1,0:T(8,128)(2,1)S(1)} %bitcast.40, bf16[4,8,640]{2,1,0:T(8,128)(2,1)S(1)} %collective-permute-done.12.refs_1_, ...), custom_call_target="tpu_custom_call" | custom-call | tf_op jit(solution)/shard_map/backward_attention/pallas_call | solution.py:417
  104.3 0.1 copy.20
  104.4 13.1 %all_to_all.19 = f32[32,1,512]{2,1,0:T(1,128)S(1)} all-to-all(f32[32,1,512]{2,1,0:T(1,128)S(1)} %copy.20), channel_id=1, replica_groups=mesh['y'=4,'z'=8,'tm'=8] {'y','tm'}, dimensions={0} | all-to-all | bytes 131072 | tf_op jit(solution)/shard_map/all_to_all | solution.py:497
  117.5 0.1 reduce_sum.9
  117.6 0.1 broadcast_in_dim.30
  117.7 22.7 %all_to_all.20 = bf16[256,4,128]{2,1,0:T(4,128)(2,1)S(1)} all-to-all(bf16[256,4,128]{2,1,0:T(4,128)(2,1)S(1)} %broadcast_in_dim.30), channel_id=1, replica_groups=mesh['y'=4,'z'=8,'tm'=8] {'y','z','tm'}, dimensions={0} | all-to-all | bytes 524288 | tf_op jit(solution)/shard_map/all_to_all | solution.py:500
  140.4 1.1 fusion
  (5 shorter events, 0.0 us)
Async XLA Ops:
  0.6 9.7 %copy-start = (bf16[512,512]{1,0:T(8,128)(2,1)S(1)}, bf16[512,512]{1,0:T(8,128)(2,1)}, u32[]{:S(2)}) copy-start(bf16[512,512]{1,0:T(8,128)(2,1)} %param.19) | copy-start | bytes 1572868
  3.1 15.7 %collective-permute-start.1 = (bf16[256,256]{1,0:T(8,128)(2,1)S(1)}, bf16[256,256]{1,0:T(8,128)(2,1)S(1)}, u32[]{:S(2)}, u32[]{:S(2)}) collective-permute-start(bf16[256,256]{1,0:T(8,128)(2,1)S(1)} %pad_maximum_fusion.refs_0_), channel_id=1, source_target_pairs={{0,56},{8,0},{16,8},{24,16},{32,24},{40,32},{48,40},{56,48},{1,57}... | collective-permute-start | bytes 393224 | tf_op jit(solution)/shard_map/ppermute | solution.py:467
  9.5 9.3 %collective-permute-start = (bf16[256,256]{1,0:T(8,128)(2,1)S(1)}, bf16[256,256]{1,0:T(8,128)(2,1)S(1)}, u32[]{:S(2)}, u32[]{:S(2)}) collective-permute-start(bf16[256,256]{1,0:T(8,128)(2,1)S(1)} %pad_maximum_fusion.refs_0_), channel_id=1, source_target_pairs={{0,8},{8,16},{16,24},{24,32},{32,40},{40,48},{48,56},{56,0},{1,9},... | collective-permute-start | bytes 393224 | tf_op jit(solution)/shard_map/ppermute | solution.py:465
  10.5 2.2 %copy-start.1 = (bf16[4096,512]{1,0:T(8,128)(2,1)S(1)}, bf16[4096,512]{1,0:T(8,128)(2,1)}, u32[]{:S(2)}) copy-start(bf16[4096,512]{1,0:T(8,128)(2,1)} %refs_4_.9) | copy-start | bytes 12582916
  12.7 1.2 copy-start.3
  13.9 0.8 copy-start.4
  14.7 7.0 %copy-start.2 = (bf16[4096,512]{1,0:T(8,128)(2,1)S(1)}, bf16[4096,512]{1,0:T(8,128)(2,1)}, u32[]{:S(2)}) copy-start(bf16[4096,512]{1,0:T(8,128)(2,1)} %refs_4_.9) | copy-start | bytes 12582916
  18.8 11.7 %collective-permute-start.2 = (bf16[256,256]{1,0:T(8,128)(2,1)S(1)}, bf16[256,256]{1,0:T(8,128)(2,1)S(1)}, u32[]{:S(2)}, u32[]{:S(2)}) collective-permute-start(bf16[256,256]{1,0:T(8,128)(2,1)S(1)} %collective-permute-done.refs_0_), channel_id=1, source_target_pairs={{0,8},{8,16},{16,24},{24,32},{32,40},{40,48},{48,56},{56,0},{1,9},... | collective-permute-start | bytes 393224 | tf_op jit(solution)/shard_map/ppermute | solution.py:465
  18.9 11.6 %collective-permute-start.3 = (bf16[256,256]{1,0:T(8,128)(2,1)S(1)}, bf16[256,256]{1,0:T(8,128)(2,1)S(1)}, u32[]{:S(2)}, u32[]{:S(2)}) collective-permute-start(bf16[256,256]{1,0:T(8,128)(2,1)S(1)} %collective-permute-done.1.refs_1_), channel_id=1, source_target_pairs={{0,56},{8,0},{16,8},{24,16},{32,24},{40,32},{48,40},{56,48},{1,57}... | collective-permute-start | bytes 393224 | tf_op jit(solution)/shard_map/ppermute | solution.py:467
  30.5 11.6 %collective-permute-start.4 = (bf16[256,256]{1,0:T(8,128)(2,1)S(1)}, bf16[256,256]{1,0:T(8,128)(2,1)S(1)}, u32[]{:S(2)}, u32[]{:S(2)}) collective-permute-start(bf16[256,256]{1,0:T(8,128)(2,1)S(1)} %collective-permute-done.2.refs_0_), channel_id=1, source_target_pairs={{0,8},{8,16},{16,24},{24,32},{32,40},{40,48},{48,56},{56,0},{1,9},... | collective-permute-start | bytes 393224 | tf_op jit(solution)/shard_map/ppermute | solution.py:465
  30.6 11.5 %collective-permute-start.5 = (bf16[256,256]{1,0:T(8,128)(2,1)S(1)}, bf16[256,256]{1,0:T(8,128)(2,1)S(1)}, u32[]{:S(2)}, u32[]{:S(2)}) collective-permute-start(bf16[256,256]{1,0:T(8,128)(2,1)S(1)} %collective-permute-done.3.refs_1_), channel_id=1, source_target_pairs={{0,56},{8,0},{16,8},{24,16},{32,24},{40,32},{48,40},{56,48},{1,57}... | collective-permute-start | bytes 393224 | tf_op jit(solution)/shard_map/ppermute | solution.py:467
  42.1 8.9 %collective-permute-start.6 = (bf16[256,256]{1,0:T(8,128)(2,1)S(1)}, bf16[256,256]{1,0:T(8,128)(2,1)S(1)}, u32[]{:S(2)}, u32[]{:S(2)}) collective-permute-start(bf16[256,256]{1,0:T(8,128)(2,1)S(1)} %collective-permute-done.4.refs_0_), channel_id=1, source_target_pairs={{0,8},{8,16},{16,24},{24,32},{32,40},{40,48},{48,56},{56,0},{1,9},... | collective-permute-start | bytes 393224 | tf_op jit(solution)/shard_map/ppermute | solution.py:465
  51.0 23.1 %copy-start.6 = (bf16[4,8,512]{2,1,0:T(8,128)(2,1)S(1)}, bf16[4,8,512]{2,1,0:T(8,128)(2,1)}, u32[]{:S(2)}) copy-start(bf16[4,8,512]{2,1,0:T(8,128)(2,1)} %param.23) | copy-start | bytes 98308
  51.0 31.8 %copy-start.5 = (bf16[512,512]{1,0:T(8,128)(2,1)S(1)}, bf16[512,512]{1,0:T(8,128)(2,1)}, u32[]{:S(2)}) copy-start(bf16[512,512]{1,0:T(8,128)(2,1)} %w_out_ref.1) | copy-start | bytes 1572868
  51.1 31.8 %copy-start.7 = (f32[2,512]{1,0:T(2,128)S(1)}, f32[2,512]{1,0:T(2,128)}, u32[]{:S(2)}) copy-start(f32[2,512]{1,0:T(2,128)} %bias_ref.1) | copy-start | bytes 12292
  56.7 4.3 %collective-permute-start.7 = (f32[4,8,640]{2,1,0:T(8,128)S(1)}, f32[4,8,640]{2,1,0:T(8,128)S(1)}, u32[]{:S(2)}, u32[]{:S(2)}) collective-permute-start(f32[4,8,640]{2,1,0:T(8,128)S(1)} %get-tuple-element.63), channel_id=1, source_target_pairs={{0,192},{64,0},{128,64},{192,128},{1,193},{65,1},{129,65},{193,129... | collective-permute-start | bytes 245768 | tf_op jit(solution)/shard_map/ppermute | solution.py:478
  59.5 4.9 %collective-permute-start.8 = (f32[4,8,640]{2,1,0:T(8,128)S(1)}, f32[4,8,640]{2,1,0:T(8,128)S(1)}, u32[]{:S(2)}, u32[]{:S(2)}) collective-permute-start(f32[4,8,640]{2,1,0:T(8,128)S(1)} %get-tuple-element.64), channel_id=1, source_target_pairs={{0,128},{64,192},{128,0},{192,64},{1,129},{65,193},{129,1},{193,65... | collective-permute-start | bytes 245768 | tf_op jit(solution)/shard_map/ppermute | solution.py:478
  60.0 5.2 %collective-permute-start.9 = (f32[4,8,640]{2,1,0:T(8,128)S(1)}, f32[4,8,640]{2,1,0:T(8,128)S(1)}, u32[]{:S(2)}, u32[]{:S(2)}) collective-permute-start(f32[4,8,640]{2,1,0:T(8,128)S(1)} %get-tuple-element.65), channel_id=1, source_target_pairs={{0,64},{64,128},{128,192},{192,0},{1,65},{65,129},{129,193},{193,1... | collective-permute-start | bytes 245768 | tf_op jit(solution)/shard_map/ppermute | solution.py:478
  66.3 16.5 %all-to-all-start = ((bf16[8,32,512]{2,1,0:T(8,128)(2,1)}), bf16[8,32,512]{2,1,0:T(8,128)(2,1)S(1)}, u32[]{:S(2)}, u32[]{:S(2)}) async-start(bf16[8,32,512]{2,1,0:T(8,128)(2,1)} %get-tuple-element.67), calls=%async_computation | async-start | bytes 524288 | tf_op jit(solution)/shard_map/all_to_all | solution.py:487
  74.1 5.5 %collective-permute-start.10 = (bf16[24,512]{1,0:T(8,128)(2,1)S(1)}, bf16[24,512]{1,0:T(8,128)(2,1)S(1)}, u32[]{:S(2)}, u32[]{:S(2)}) collective-permute-start(bf16[24,512]{1,0:T(8,128)(2,1)S(1)} %get-tuple-element.69), channel_id=1, source_target_pairs={{0,1},{1,2},{2,3},{3,4},{4,5},{5,6},{6,7},{8,9},{9,10},{10,11},{11... | collective-permute-start | bytes 73736 | tf_op jit(solution)/shard_map/ppermute | solution.py:482
  77.7 5.1 %collective-permute-start.11 = (bf16[24,512]{1,0:T(8,128)(2,1)S(1)}, bf16[24,512]{1,0:T(8,128)(2,1)S(1)}, u32[]{:S(2)}, u32[]{:S(2)}) collective-permute-start(bf16[24,512]{1,0:T(8,128)(2,1)S(1)} %get-tuple-element.70), channel_id=1, source_target_pairs={{1,0},{2,1},{3,2},{4,3},{5,4},{6,5},{7,6},{9,8},{10,9},{11,10},{12... | collective-permute-start | bytes 73736 | tf_op jit(solution)/shard_map/ppermute | solution.py:483
  88.4 3.2 %collective-permute-start.14 = (bf16[4,8,640]{2,1,0:T(8,128)(2,1)S(1)}, bf16[4,8,640]{2,1,0:T(8,128)(2,1)S(1)}, u32[]{:S(2)}, u32[]{:S(2)}) collective-permute-start(bf16[4,8,640]{2,1,0:T(8,128)(2,1)S(1)} %bitcast.37), channel_id=1, source_target_pairs={{0,192},{64,0},{128,64},{192,128},{1,193},{65,1},{129,65},{193,129... | collective-permute-start | bytes 122888 | tf_op jit(solution)/shard_map/ppermute | solution.py:494
  88.7 4.4 %collective-permute-start.13 = (bf16[4,8,640]{2,1,0:T(8,128)(2,1)S(1)}, bf16[4,8,640]{2,1,0:T(8,128)(2,1)S(1)}, u32[]{:S(2)}, u32[]{:S(2)}) collective-permute-start(bf16[4,8,640]{2,1,0:T(8,128)(2,1)S(1)} %bitcast.38), channel_id=1, source_target_pairs={{0,128},{64,192},{128,0},{192,64},{1,129},{65,193},{129,1},{193,65... | collective-permute-start | bytes 122888 | tf_op jit(solution)/shard_map/ppermute | solution.py:494
  89.4 4.7 %collective-permute-start.12 = (bf16[4,8,640]{2,1,0:T(8,128)(2,1)S(1)}, bf16[4,8,640]{2,1,0:T(8,128)(2,1)S(1)}, u32[]{:S(2)}, u32[]{:S(2)}) collective-permute-start(bf16[4,8,640]{2,1,0:T(8,128)(2,1)S(1)} %bitcast.39), channel_id=1, source_target_pairs={{0,64},{64,128},{128,192},{192,0},{1,65},{65,129},{129,193},{193,1... | collective-permute-start | bytes 122888 | tf_op jit(solution)/shard_map/ppermute | solution.py:494
where the time goes:
time: 142 us
  Pallas kernels  53.1 us (37%)
  blocking collectives  35.8 us (25%)
  starting transfers between devices  31.1 us (22%)
  waiting for transfers between devices  11.8 us (8%)
  local copies, waits for them, and re-layouts  5.12 us (4%)
  other arithmetic  1.76 us (1%)
  between operations  1.57 us (1%)
    pallas_call x5, Pallas kernels, absorb(): pl.pallas_call(functools.partial(absorb_kernel, fresh=fresh, last=last, c...  36.2 us
    all_to_all x1, blocking collectives, local(): dq_all = lax.all_to_all(spread, ('y', 'z', 'tm'), 0, 0, tiled=True)  22.7 us
    all_to_all x1, blocking collectives, local(): pieces = lax.all_to_all(dq, ('y', 'tm'), 0, 0, tiled=True)  13.1 us
    ppermute x3, starting transfers between devices, local(): above = lax.ppermute(above, 'z', shift(NZ, -1))  11.9 us
    pallas_call x1, Pallas kernels, backward_attention(): pl.pallas_call(functools.partial(backward_kernel, slots=len(msgs)), in_sp...  10.2 us
    all_to_all x1, starting transfers between devices, local(): everyone = lax.all_to_all(copies, 'tm', 0, 0)  7.83 us
    pallas_call x1, Pallas kernels, conv_stack(): pl.pallas_call(conv_kernel, in_specs=[pl.BlockSpec(memory_space=pltpu.SME...  5.53 us
    ppermute x3, waiting for transfers between devices, local(): lax.ppermute(parts[s], 'y', shift(NY, -s))  4.63 us
  transfers between devices with their start and end apart: 16, of which 7 were waited for; matrix products, arithmetic and copies ran while one was open for 1% of the time, Pallas kernels for 22%

commit v1 on v0

--- a/solution.py
+++ b/solution.py
@@ -80,6 +80,81 @@
 
 def rounded(value):
     return value.astype(bf16).astype(f32)
+
+
+def message_kernel(live_ref, signal_hbm, index_hbm, message_ref, signal_ref, index_ref, sem):
+    con_dev, span = signal_hbm.shape
+    copies = [
+        pltpu.make_async_copy(index_hbm, index_ref, sem.at[0]),
+        pltpu.make_async_copy(signal_hbm, signal_ref, sem.at[1]),
+    ]
+    for copy in copies:
+        copy.start()
+    copies[0].wait()
+    index = index_ref[...].astype(f32)
+    for r in range(con_dev // 128):
+        column = jnp.transpose(jnp.broadcast_to(index[r : r + 1], (128, 128)))
+        high = jnp.floor(column * (1.0 / 64.0))
+        lane = lax.broadcasted_iota(jnp.int32, column.shape, 1)
+        meta = jnp.where(lane == 0, high, jnp.where(lane == 1, column - 64.0 * high, live_ref[0].astype(f32)))
+        message_ref[r * 128 : (r + 1) * 128, span:] = meta.astype(bf16)
+    copies[1].wait()
+    message_ref[:, :span] = signal_ref[...]
+
+
+def make_message(live_count, signal, pos_idx):
+    con_dev, span = signal.shape
+    index = pos_idx.reshape(con_dev // 128, 128)
+    signal, index = (pltpu.with_memory_space_constraint(a, pltpu.HBM) for a in (signal, index))
+    hbm = pl.BlockSpec(memory_space=pltpu.HBM)
+    return pl.pallas_call(
+        message_kernel,
+        in_specs=[pl.BlockSpec(memory_space=pltpu.SMEM), hbm, hbm],
+        out_specs=pl.BlockSpec(memory_space=pltpu.VMEM),
+        out_shape=jax.ShapeDtypeStruct((con_dev, span + 128), bf16),
+        scratch_shapes=[
+            pltpu.VMEM(signal.shape, signal.dtype),
+            pltpu.VMEM(index.shape, index.dtype),
+            pltpu.SemaphoreType.DMA((2,)),
+        ],
+        compiler_params=pltpu.CompilerParams(vmem_limit_bytes=8 * MIB),
+        name="make_message",
+    )(live_count, signal, index)
+
+
+def prepare_kernel(y_ref, z_ref, *refs):
+    hbms, (q_ref, *here), sem = refs[:5], refs[5:11], refs[11]
+    latents_ref, w_query_ref = here[3], here[4]
+    copies = [pltpu.make_async_copy(a, b, sem.at[i]) for i, (a, b) in enumerate(zip(hbms, here))]
+    for i in (3, 4, 0, 1, 2):
+        copies[i].start()
+    lat, each = latents_ref.shape[0], latents_ref.shape[0] // (NY * NZ)
+    row = lax.broadcasted_iota(jnp.int32, (q_ref.shape[0], lat), 0)
+    owner = (y_ref[0] + NY - row // each) % NY
+    place = (owner * NZ + z_ref[0]) * each + row % each
+    pick = jnp.where(lax.broadcasted_iota(jnp.int32, row.shape, 1) == place, 1.0, 0.0).astype(bf16)
+    copies[3].wait()
+    chosen = nn_dot(pick, latents_ref[...]).astype(bf16)
+    copies[4].wait()
+    q_ref[...] = nn_dot(chosen, w_query_ref[...]).astype(bf16)
+    for copy in copies[:3]:
+        copy.wait()
+
+
+def prepare(y, z, table, w_kv, w_in, latents, w_query):
+    smem, vmem = pl.BlockSpec(memory_space=pltpu.SMEM), pl.BlockSpec(memory_space=pltpu.VMEM)
+    arrays = [pltpu.with_memory_space_constraint(a, pltpu.HBM) for a in (table, w_kv, w_in, latents, w_query)]
+    return pl.pallas_call(
+        prepare_kernel,
+        in_specs=[smem] * 2 + [pl.BlockSpec(memory_space=pltpu.HBM)] * 5,
+        out_specs=[vmem] * 4,
+        out_shape=[jax.ShapeDtypeStruct((latents.shape[0] // NZ, w_query.shape[1]), bf16)]
+        + [pltpu.VMEM(a.shape, a.dtype) for a in (table, w_kv, w_in)],
+        scratch_shapes=[pltpu.VMEM(a.shape, a.dtype) for a in (latents, w_query)]
+        + [pltpu.SemaphoreType.DMA((5,))],
+        compiler_params=pltpu.CompilerParams(vmem_limit_bytes=8 * MIB),
+        name="prepare",
+    )(y, z, *arrays)
 
 
 def absorb_kernel(*refs, fresh, last, count):
@@ -273,8 +348,6 @@
     weights = [pltpu.make_async_copy(conv_hbm.at[l], conv_ref.at[l], sem.at[l]) for l in range(LAYERS)]
     for copy in weights:
         copy.start()
-    for copy in fetches:
-        copy.start()
     rows, width = own_ref.shape
     heads = width // HD
     windows = 4
@@ -301,6 +374,8 @@
     x1 = jnp.where(inside(1, 14), x1, 0.0)
     n1 = 10 * each
     weights[1].wait()
+    for copy in fetches:
+        copy.start()
     pre1 = bias_ref[1:2, :] + sum(nn_dot(x1[2 * j * each : 2 * j * each + n1].astype(bf16), conv_ref[1, j]) for j in range(KSIZE))
     feat_ref[...] = (x1[5 * each : 9 * each] + jax.nn.silu(pre1[3 * each : 7 * each])).astype(bf16)
     g2 = jnp.concatenate([r[...].astype(f32) for r in (cl_ref, cot_ref, cr_ref)], axis=0)
@@ -446,18 +521,13 @@
     up1 = [(i, i + 1) for i in range(NTM - 1)]
     down1 = [(i + 1, i) for i in range(NTM - 1)]
 
-    by_owner = latents.reshape(NY, NZ, lat_dev, width)
-    mine = lax.dynamic_index_in_dim(by_owner, z, 1, False)
-    slots = jnp.stack([lax.dynamic_index_in_dim(mine, (y + NY - s) % NY, 0, False) for s in range(NY)])
-    queries = nn_dot(slots.reshape(NY * lat_dev, width), w_query).astype(bf16)
-
-    lane = lax.broadcasted_iota(jnp.int32, (con_dev, 128), 1)
-    index = pos_idx[:, None]
-    meta = jnp.where(lane == 0, index // 64, jnp.where(lane == 1, index % 64, live_count[0]))
-    own = jnp.concatenate([signal, meta.astype(bf16)], axis=1)
+    own = make_message(live_count, signal, pos_idx)
+    queries, table, kv_weights, in_weights = prepare(
+        y.reshape(1), z.reshape(1), pos_table, w_kv, w_in, latents, w_query
+    )
 
     def absorbed(messages, state, last=False):
-        return absorb(messages, queries, w_in, w_kv, pos_table, state, last)
+        return absorb(messages, queries, in_weights, kv_weights, table, state, last)
 
     below, above = own, own
     at_hand, state, kvs, valids = [own], None, [], []

time: 142 us -> 140 us (0.986)
  local copies, waits for them, and re-layouts: 5.12 us -> 0.17 us
  Pallas kernels: 53.1 us -> 56 us
  blocking collectives: 35.8 us -> 38.4 us
  other arithmetic: 1.76 us -> 0.07 us
    unnamed x16 -> x8, local copies, waits for them, and re-layouts: 4.22 us -> 0.02 us
    pallas_call x0 -> x2, Pallas kernels: none -> 3.66 us  [the longest x1 2.77 us: prepare(): pl.pallas_call(prepare_kernel, in_specs=[smem] * 2 + [pl.BlockSpec(memory...]
    ppermute x3, starting transfers between devices: 11.9 us -> 9.35 us  [local(): above = lax.ppermute(above, 'z', shift(NZ, -1))]
    ppermute x4, starting transfers between devices: 0.25 us -> 2.78 us  [local(): below = lax.ppermute(below, 'z', shift(NZ, 1))]
  transfers between devices with their start and end apart: 16 -> 16, of which waited for: 7 -> 6; matrix products, arithmetic and copies ran while one was open for 1% -> 0% of each run, Pallas kernels for 22% -> 24%
where the time goes in v1:
time: 140 us
  Pallas kernels  56 us (40%)
  blocking collectives  38.4 us (27%)
  starting transfers between devices  32.3 us (23%)
  waiting for transfers between devices  10.4 us (7%)
  between operations  1.52 us (1%)
    pallas_call x5, Pallas kernels, absorb(): pl.pallas_call(functools.partial(absorb_kernel, fresh=fresh, last=last, c...  36.1 us
    all_to_all x1, blocking collectives, local(): dq_all = lax.all_to_all(spread, ('y', 'z', 'tm'), 0, 0, tiled=True)  23.9 us
    all_to_all x1, blocking collectives, local(): pieces = lax.all_to_all(dq, ('y', 'tm'), 0, 0, tiled=True)  14.5 us
    pallas_call x1, Pallas kernels, backward_attention(): pl.pallas_call(functools.partial(backward_kernel, slots=len(msgs)), in_sp...  10.2 us
    ppermute x3, starting transfers between devices, local(): above = lax.ppermute(above, 'z', shift(NZ, -1))  9.35 us
    all_to_all x1, starting transfers between devices, local(): everyone = lax.all_to_all(copies, 'tm', 0, 0)  7.82 us
    pallas_call x1, Pallas kernels, conv_stack(): pl.pallas_call(conv_kernel, in_specs=[pl.BlockSpec(memory_space=pltpu.SME...  4.83 us
    ppermute x3, waiting for transfers between devices, local(): lax.ppermute(parts[s], 'y', shift(NY, -s))  4.63 us
  transfers between devices with their start and end apart: 16, of which 6 were waited for; matrix products, arithmetic and copies ran while one was open for 0% of the time, Pallas kernels for 24%

profile of v1, /device:TPU:1, one launch (start us, length us, event | category | flops | bytes accessed | tf_op | source)
XLA Modules:
  0.0 139.9 jit_solution(11251798160779372880)
XLA Ops:
  1.3 0.9 make_message.1.refs_0_
  2.2 2.5 %collective-permute-start = (bf16[256,256]{1,0:T(8,128)(2,1)S(1)}, bf16[256,256]{1,0:T(8,128)(2,1)S(1)}, u32[]{:S(2)}, u32[]{:S(2)}) collective-permute-start(bf16[256,256]{1,0:T(8,128)(2,1)S(1)} %make_message.1.refs_0_), channel_id=1, source_target_pairs={{0,8},{8,16},{16,24},{24,32},{32,40},{40,48},{48,56},{56,0},{1,9},... | collective-permute-start | bytes 393224 | tf_op jit(solution)/shard_map/ppermute | solution.py:535
  4.7 4.0 %collective-permute-start.1 = (bf16[256,256]{1,0:T(8,128)(2,1)S(1)}, bf16[256,256]{1,0:T(8,128)(2,1)S(1)}, u32[]{:S(2)}, u32[]{:S(2)}) collective-permute-start(bf16[256,256]{1,0:T(8,128)(2,1)S(1)} %make_message.1.refs_0_), channel_id=1, source_target_pairs={{0,56},{8,0},{16,8},{24,16},{32,24},{40,32},{48,40},{56,48},{1,57}... | collective-permute-start | bytes 393224 | tf_op jit(solution)/shard_map/ppermute | solution.py:537
  8.7 2.8 %prepare.1 = (bf16[32,512]{1,0:T(8,128)(2,1)S(1)}, bf16[4096,512]{1,0:T(8,128)(2,1)S(1)}, bf16[512,1024]{1,0:T(8,128)(2,1)S(1)}, bf16[32,512]{1,0:T(8,128)(2,1)S(1)}) custom-call(s32[1]{0:T(128)} %bitcast.2.y_ref, s32[1]{0:T(128)} %bitcast.3.z_ref, bf16[4096,512]{1,0:T(8,128)(2,1)} %refs_0_.1, bf16[512,1024]{1,0:T(8,128)(2,1)} %refs_1_.1, ...), custom_call_target="tpu_custom_call" | custom-call | tf_op jit(solution)/shard_map/prepare/pallas_call | solution.py:147
  11.5 4.1 %absorb.5 = (bf16[4,256,1024]{2,1,0:T(8,128)(2,1)}, f32[8,256]{1,0:T(8,128)S(1)}, f32[4,256,512]{2,1,0:T(8,128)S(1)}, f32[4,256,128]{2,1,0:T(8,128)S(1)}) custom-call(bf16[256,256]{1,0:T(8,128)(2,1)S(1)} %make_message.1.refs_0_, bf16[32,512]{1,0:T(8,128)(2,1)S(1)} %get-tuple-element.49.refs_1_.refs_2_.q_ref, ...), custom_call_target="tpu_custom_call" | custom-call | tf_op jit(solution)/shard_map/absorb/pallas_call | solution.py:281
  15.6 0.0 collective-permute-done.refs_0_
  15.6 0.0 collective-permute-done.1.refs_1_
  15.6 0.1 collective-permute-start.2
  15.7 2.7 %collective-permute-start.3 = (bf16[256,256]{1,0:T(8,128)(2,1)S(1)}, bf16[256,256]{1,0:T(8,128)(2,1)S(1)}, u32[]{:S(2)}, u32[]{:S(2)}) collective-permute-start(bf16[256,256]{1,0:T(8,128)(2,1)S(1)} %collective-permute-done.1.refs_1_), channel_id=1, source_target_pairs={{0,56},{8,0},{16,8},{24,16},{32,24},{40,32},{48,40},{56,48},{1,57}... | collective-permute-start | bytes 393224 | tf_op jit(solution)/shard_map/ppermute | solution.py:537
  18.4 8.8 %absorb.6 = (bf16[4,512,1024]{2,1,0:T(8,128)(2,1)}, f32[8,512]{1,0:T(8,128)S(1)}, f32[4,256,512]{2,1,0:T(8,128)S(1)}, f32[4,256,128]{2,1,0:T(8,128)S(1)}) custom-call(bf16[256,256]{1,0:T(8,128)(2,1)S(1)} %collective-permute-done.refs_0_, bf16[256,256]{1,0:T(8,128)(2,1)S(1)} %collective-permute-done.1.refs_1_, ...), custom_call_target="tpu_custom_call", output_to_operand_aliasing={{2}: (6, {}), {3}: (7, {})} | custom-call | tf_op jit(solution)/shard_map/absorb/pallas_call | solution.py:281
  27.2 0.0 collective-permute-done.2.refs_0_
  27.2 0.0 collective-permute-done.3.refs_1_
  27.2 0.1 collective-permute-start.4
  27.3 2.7 %collective-permute-start.5 = (bf16[256,256]{1,0:T(8,128)(2,1)S(1)}, bf16[256,256]{1,0:T(8,128)(2,1)S(1)}, u32[]{:S(2)}, u32[]{:S(2)}) collective-permute-start(bf16[256,256]{1,0:T(8,128)(2,1)S(1)} %collective-permute-done.3.refs_1_), channel_id=1, source_target_pairs={{0,56},{8,0},{16,8},{24,16},{32,24},{40,32},{48,40},{56,48},{1,57}... | collective-permute-start | bytes 393224 | tf_op jit(solution)/shard_map/ppermute | solution.py:537
  30.0 8.8 %absorb.7 = (bf16[4,512,1024]{2,1,0:T(8,128)(2,1)}, f32[8,512]{1,0:T(8,128)S(1)}, f32[4,256,512]{2,1,0:T(8,128)S(1)}, f32[4,256,128]{2,1,0:T(8,128)S(1)}) custom-call(bf16[256,256]{1,0:T(8,128)(2,1)S(1)} %collective-permute-done.2.refs_0_, bf16[256,256]{1,0:T(8,128)(2,1)S(1)} %collective-permute-done.3.refs_1_, ...), custom_call_target="tpu_custom_call", output_to_operand_aliasing={{2}: (6, {}), {3}: (7, {})} | custom-call | tf_op jit(solution)/shard_map/absorb/pallas_call | solution.py:281
  38.8 0.0 collective-permute-done.4.refs_0_
  38.8 0.0 collective-permute-done.5.refs_1_
  38.8 0.1 collective-permute-start.6
  38.9 8.8 %absorb.8 = (bf16[4,512,1024]{2,1,0:T(8,128)(2,1)}, f32[8,512]{1,0:T(8,128)S(1)}, f32[4,256,512]{2,1,0:T(8,128)S(1)}, f32[4,256,128]{2,1,0:T(8,128)S(1)}) custom-call(bf16[256,256]{1,0:T(8,128)(2,1)S(1)} %collective-permute-done.4.refs_0_, bf16[256,256]{1,0:T(8,128)(2,1)S(1)} %collective-permute-done.5.refs_1_, ...), custom_call_target="tpu_custom_call", output_to_operand_aliasing={{2}: (6, {}), {3}: (7, {})} | custom-call | tf_op jit(solution)/shard_map/absorb/pallas_call | solution.py:281
  47.7 0.0 collective-permute-done.6.refs_0_
  47.7 0.0 copy-start.1
  47.8 0.0 copy-start
  47.8 0.0 copy-start.2
  47.8 5.6 %absorb.9 = (bf16[4,256,1024]{2,1,0:T(8,128)(2,1)}, f32[8,256]{1,0:T(8,128)S(1)}, f32[4,8,640]{2,1,0:T(8,128)S(1)}, f32[4,8,640]{2,1,0:T(8,128)S(1)}, f32[4,8,64...) custom-call(bf16[256,256]{1,0:T(8,128)(2,1)S(1)} %collective-permute-done.6.refs_0_, ...), custom_call_target="tpu_custom_call" | custom-call | tf_op jit(solution)/shard_map/absorb/pallas_call | solution.py:281
  53.4 2.8 %collective-permute-start.7 = (f32[4,8,640]{2,1,0:T(8,128)S(1)}, f32[4,8,640]{2,1,0:T(8,128)S(1)}, u32[]{:S(2)}, u32[]{:S(2)}) collective-permute-start(f32[4,8,640]{2,1,0:T(8,128)S(1)} %get-tuple-element.71), channel_id=1, source_target_pairs={{0,192},{64,0},{128,64},{192,128},{1,193},{65,1},{129,65},{193,129... | collective-permute-start | bytes 245768 | tf_op jit(solution)/shard_map/ppermute | solution.py:548
  56.2 0.5 collective-permute-start.8
  56.7 0.5 collective-permute-start.9
  57.2 0.4 collective-permute-done.7.refs_1_
  57.7 3.4 %collective-permute-done.8.refs_2_ = f32[4,8,640]{2,1,0:T(8,128)S(1)} collective-permute-done((f32[4,8,640]{2,1,0:T(8,128)S(1)}, f32[4,8,640]{2,1,0:T(8,128)S(1)}, u32[]{:S(2)}, u32[]{:S(2)}) %collective-permute-start.8) | collective-permute-done | bytes 81952 | tf_op jit(solution)/shard_map/ppermute | solution.py:548
  61.1 0.8 collective-permute-done.9.refs_3_
  61.9 1.1 combine_parts.1
  63.0 7.8 %all-to-all-start = ((bf16[8,32,512]{2,1,0:T(8,128)(2,1)}), bf16[8,32,512]{2,1,0:T(8,128)(2,1)S(1)}, u32[]{:S(2)}, u32[]{:S(2)}) async-start(bf16[8,32,512]{2,1,0:T(8,128)(2,1)} %get-tuple-element.75), calls=%async_computation | async-start | bytes 524288 | tf_op jit(solution)/shard_map/all_to_all | solution.py:557
  70.8 0.0 copy-done.1
  70.8 3.5 %collective-permute-start.10 = (bf16[24,512]{1,0:T(8,128)(2,1)S(1)}, bf16[24,512]{1,0:T(8,128)(2,1)S(1)}, u32[]{:S(2)}, u32[]{:S(2)}) collective-permute-start(bf16[24,512]{1,0:T(8,128)(2,1)S(1)} %get-tuple-element.77), channel_id=1, source_target_pairs={{0,1},{1,2},{2,3},{3,4},{4,5},{5,6},{6,7},{8,9},{9,10},{10,11},{11... | collective-permute-start | bytes 73736 | tf_op jit(solution)/shard_map/ppermute | solution.py:552
  74.4 1.9 %collective-permute-start.11 = (bf16[24,512]{1,0:T(8,128)(2,1)S(1)}, bf16[24,512]{1,0:T(8,128)(2,1)S(1)}, u32[]{:S(2)}, u32[]{:S(2)}) collective-permute-start(bf16[24,512]{1,0:T(8,128)(2,1)S(1)} %get-tuple-element.78), channel_id=1, source_target_pairs={{1,0},{2,1},{3,2},{4,3},{5,4},{6,5},{7,6},{9,8},{10,9},{11,10},{12... | collective-permute-start | bytes 73736 | tf_op jit(solution)/shard_map/ppermute | solution.py:553
  76.3 0.0 collective-permute-done.10.cl_ref
  76.3 3.2 %collective-permute-done.11.cr_ref = bf16[24,512]{1,0:T(8,128)(2,1)S(1)} collective-permute-done((bf16[24,512]{1,0:T(8,128)(2,1)S(1)}, bf16[24,512]{1,0:T(8,128)(2,1)S(1)}, u32[]{:S(2)}, u32[]{:S(2)}) %collective-permute-start.11) | collective-permute-done | bytes 24608 | tf_op jit(solution)/shard_map/ppermute | solution.py:553
  79.5 0.0 all-to-all-done
  79.5 0.0 copy-done
  79.5 0.0 copy-done.2
  79.5 4.8 %conv_stack.1 = (bf16[32,512]{1,0:T(8,128)(2,1)}, bf16[32,640]{1,0:T(8,128)(2,1)S(1)}, bf16[256,1024]{1,0:T(8,128)(2,1)S(1)}, bf16[512,1024]{1,0:T(8,128)(2,1)S(...) custom-call(s32[1]{0:T(128)} %bitcast.tm_ref, ...), custom_call_target="tpu_custom_call" | custom-call | tf_op jit(solution)/shard_map/conv_stack/pallas_call | solution.py:414
  84.4 0.1 collective-permute-start.12
  84.5 1.5 %collective-permute-start.13 = (bf16[4,8,640]{2,1,0:T(8,128)(2,1)S(1)}, bf16[4,8,640]{2,1,0:T(8,128)(2,1)S(1)}, u32[]{:S(2)}, u32[]{:S(2)}) collective-permute-start(bf16[4,8,640]{2,1,0:T(8,128)(2,1)S(1)} %bitcast.25), channel_id=1, source_target_pairs={{0,128},{64,192},{128,0},{192,64},{1,129},{65,193},{129,1},{193,65... | collective-permute-start | bytes 122888 | tf_op jit(solution)/shard_map/ppermute | solution.py:564
  85.9 1.5 %collective-permute-start.14 = (bf16[4,8,640]{2,1,0:T(8,128)(2,1)S(1)}, bf16[4,8,640]{2,1,0:T(8,128)(2,1)S(1)}, u32[]{:S(2)}, u32[]{:S(2)}) collective-permute-start(bf16[4,8,640]{2,1,0:T(8,128)(2,1)S(1)} %bitcast.26), channel_id=1, source_target_pairs={{0,192},{64,0},{128,64},{192,128},{1,193},{65,1},{129,65},{193,129... | collective-permute-start | bytes 122888 | tf_op jit(solution)/shard_map/ppermute | solution.py:564
  87.4 1.7 %collective-permute-done.12.refs_1_ = bf16[4,8,640]{2,1,0:T(8,128)(2,1)S(1)} collective-permute-done((bf16[4,8,640]{2,1,0:T(8,128)(2,1)S(1)}, bf16[4,8,640]{2,1,0:T(8,128)(2,1)S(1)}, u32[]{:S(2)}, u32[]{:S(2)}) %collective-permute-start.12) | collective-permute-done | bytes 40992 | tf_op jit(solution)/shard_map/ppermute | solution.py:564
  89.1 0.0 collective-permute-done.13.refs_2_
  89.1 0.9 collective-permute-done.14.refs_3_
  89.9 0.0 copy-start.3
  89.9 10.2 %backward_attention.1 = f32[32,512]{1,0:T(8,128)S(1)} custom-call(s32[1]{0:T(128)} %bitcast.2.y_ref, bf16[32,512]{1,0:T(8,128)(2,1)S(1)} %get-tuple-element.49.refs_1_.refs_2_.q_ref, bf16[4,8,640]{2,1,0:T(8,128)(2,1)S(1)} %bitcast.27, bf16[4,8,640]{2,1,0:T(8,128)(2,1)S(1)} %collective-permute-done.12.refs_1_, ...), custom_call_target="tpu_custom_call" | custom-call | tf_op jit(solution)/shard_map/backward_attention/pallas_call | solution.py:492
  100.2 0.1 copy.20
  100.2 14.5 %all_to_all.19 = f32[32,1,512]{2,1,0:T(1,128)S(1)} all-to-all(f32[32,1,512]{2,1,0:T(1,128)S(1)} %copy.20), channel_id=1, replica_groups=mesh['y'=4,'z'=8,'tm'=8] {'y','tm'}, dimensions={0} | all-to-all | bytes 131072 | tf_op jit(solution)/shard_map/all_to_all | solution.py:567
  114.7 0.1 reduce_sum.9
  114.8 0.1 broadcast_in_dim.2
  114.8 23.9 %all_to_all.20 = bf16[256,4,128]{2,1,0:T(4,128)(2,1)S(1)} all-to-all(bf16[256,4,128]{2,1,0:T(4,128)(2,1)S(1)} %broadcast_in_dim.2), channel_id=1, replica_groups=mesh['y'=4,'z'=8,'tm'=8] {'y','z','tm'}, dimensions={0} | all-to-all | bytes 524288 | tf_op jit(solution)/shard_map/all_to_all | solution.py:570
  138.8 0.0 copy-done.3
  138.8 1.1 fusion
  (1 shorter events, 0.0 us)
Async XLA Ops:
  2.2 13.5 %collective-permute-start = (bf16[256,256]{1,0:T(8,128)(2,1)S(1)}, bf16[256,256]{1,0:T(8,128)(2,1)S(1)}, u32[]{:S(2)}, u32[]{:S(2)}) collective-permute-start(bf16[256,256]{1,0:T(8,128)(2,1)S(1)} %make_message.1.refs_0_), channel_id=1, source_target_pairs={{0,8},{8,16},{16,24},{24,32},{32,40},{40,48},{48,56},{56,0},{1,9},... | collective-permute-start | bytes 393224 | tf_op jit(solution)/shard_map/ppermute | solution.py:535
  4.7 10.9 %collective-permute-start.1 = (bf16[256,256]{1,0:T(8,128)(2,1)S(1)}, bf16[256,256]{1,0:T(8,128)(2,1)S(1)}, u32[]{:S(2)}, u32[]{:S(2)}) collective-permute-start(bf16[256,256]{1,0:T(8,128)(2,1)S(1)} %make_message.1.refs_0_), channel_id=1, source_target_pairs={{0,56},{8,0},{16,8},{24,16},{32,24},{40,32},{48,40},{56,48},{1,57}... | collective-permute-start | bytes 393224 | tf_op jit(solution)/shard_map/ppermute | solution.py:537
  15.6 11.6 %collective-permute-start.2 = (bf16[256,256]{1,0:T(8,128)(2,1)S(1)}, bf16[256,256]{1,0:T(8,128)(2,1)S(1)}, u32[]{:S(2)}, u32[]{:S(2)}) collective-permute-start(bf16[256,256]{1,0:T(8,128)(2,1)S(1)} %collective-permute-done.refs_0_), channel_id=1, source_target_pairs={{0,8},{8,16},{16,24},{24,32},{32,40},{40,48},{48,56},{56,0},{1,9},... | collective-permute-start | bytes 393224 | tf_op jit(solution)/shard_map/ppermute | solution.py:535
  15.7 11.5 %collective-permute-start.3 = (bf16[256,256]{1,0:T(8,128)(2,1)S(1)}, bf16[256,256]{1,0:T(8,128)(2,1)S(1)}, u32[]{:S(2)}, u32[]{:S(2)}) collective-permute-start(bf16[256,256]{1,0:T(8,128)(2,1)S(1)} %collective-permute-done.1.refs_1_), channel_id=1, source_target_pairs={{0,56},{8,0},{16,8},{24,16},{32,24},{40,32},{48,40},{56,48},{1,57}... | collective-permute-start | bytes 393224 | tf_op jit(solution)/shard_map/ppermute | solution.py:537
  27.2 11.6 %collective-permute-start.4 = (bf16[256,256]{1,0:T(8,128)(2,1)S(1)}, bf16[256,256]{1,0:T(8,128)(2,1)S(1)}, u32[]{:S(2)}, u32[]{:S(2)}) collective-permute-start(bf16[256,256]{1,0:T(8,128)(2,1)S(1)} %collective-permute-done.2.refs_0_), channel_id=1, source_target_pairs={{0,8},{8,16},{16,24},{24,32},{32,40},{40,48},{48,56},{56,0},{1,9},... | collective-permute-start | bytes 393224 | tf_op jit(solution)/shard_map/ppermute | solution.py:535
  27.3 11.5 %collective-permute-start.5 = (bf16[256,256]{1,0:T(8,128)(2,1)S(1)}, bf16[256,256]{1,0:T(8,128)(2,1)S(1)}, u32[]{:S(2)}, u32[]{:S(2)}) collective-permute-start(bf16[256,256]{1,0:T(8,128)(2,1)S(1)} %collective-permute-done.3.refs_1_), channel_id=1, source_target_pairs={{0,56},{8,0},{16,8},{24,16},{32,24},{40,32},{48,40},{56,48},{1,57}... | collective-permute-start | bytes 393224 | tf_op jit(solution)/shard_map/ppermute | solution.py:537
  38.8 8.9 %collective-permute-start.6 = (bf16[256,256]{1,0:T(8,128)(2,1)S(1)}, bf16[256,256]{1,0:T(8,128)(2,1)S(1)}, u32[]{:S(2)}, u32[]{:S(2)}) collective-permute-start(bf16[256,256]{1,0:T(8,128)(2,1)S(1)} %collective-permute-done.4.refs_0_), channel_id=1, source_target_pairs={{0,8},{8,16},{16,24},{24,32},{32,40},{40,48},{48,56},{56,0},{1,9},... | collective-permute-start | bytes 393224 | tf_op jit(solution)/shard_map/ppermute | solution.py:535
  47.7 23.1 %copy-start.1 = (bf16[4,8,512]{2,1,0:T(8,128)(2,1)S(1)}, bf16[4,8,512]{2,1,0:T(8,128)(2,1)}, u32[]{:S(2)}) copy-start(bf16[4,8,512]{2,1,0:T(8,128)(2,1)} %param.23) | copy-start | bytes 98308
  47.8 31.8 %copy-start = (bf16[512,512]{1,0:T(8,128)(2,1)S(1)}, bf16[512,512]{1,0:T(8,128)(2,1)}, u32[]{:S(2)}) copy-start(bf16[512,512]{1,0:T(8,128)(2,1)} %w_out_ref.1) | copy-start | bytes 1572868
  47.8 31.7 %copy-start.2 = (f32[2,512]{1,0:T(2,128)S(1)}, f32[2,512]{1,0:T(2,128)}, u32[]{:S(2)}) copy-start(f32[2,512]{1,0:T(2,128)} %bias_ref.1) | copy-start | bytes 12292
  53.4 4.3 %collective-permute-start.7 = (f32[4,8,640]{2,1,0:T(8,128)S(1)}, f32[4,8,640]{2,1,0:T(8,128)S(1)}, u32[]{:S(2)}, u32[]{:S(2)}) collective-permute-start(f32[4,8,640]{2,1,0:T(8,128)S(1)} %get-tuple-element.71), channel_id=1, source_target_pairs={{0,192},{64,0},{128,64},{192,128},{1,193},{65,1},{129,65},{193,129... | collective-permute-start | bytes 245768 | tf_op jit(solution)/shard_map/ppermute | solution.py:548
  56.2 4.9 %collective-permute-start.8 = (f32[4,8,640]{2,1,0:T(8,128)S(1)}, f32[4,8,640]{2,1,0:T(8,128)S(1)}, u32[]{:S(2)}, u32[]{:S(2)}) collective-permute-start(f32[4,8,640]{2,1,0:T(8,128)S(1)} %get-tuple-element.72), channel_id=1, source_target_pairs={{0,128},{64,192},{128,0},{192,64},{1,129},{65,193},{129,1},{193,65... | collective-permute-start | bytes 245768 | tf_op jit(solution)/shard_map/ppermute | solution.py:548
  56.7 5.2 %collective-permute-start.9 = (f32[4,8,640]{2,1,0:T(8,128)S(1)}, f32[4,8,640]{2,1,0:T(8,128)S(1)}, u32[]{:S(2)}, u32[]{:S(2)}) collective-permute-start(f32[4,8,640]{2,1,0:T(8,128)S(1)} %get-tuple-element.73), channel_id=1, source_target_pairs={{0,64},{64,128},{128,192},{192,0},{1,65},{65,129},{129,193},{193,1... | collective-permute-start | bytes 245768 | tf_op jit(solution)/shard_map/ppermute | solution.py:548
  63.0 16.5 %all-to-all-start = ((bf16[8,32,512]{2,1,0:T(8,128)(2,1)}), bf16[8,32,512]{2,1,0:T(8,128)(2,1)S(1)}, u32[]{:S(2)}, u32[]{:S(2)}) async-start(bf16[8,32,512]{2,1,0:T(8,128)(2,1)} %get-tuple-element.75), calls=%async_computation | async-start | bytes 524288 | tf_op jit(solution)/shard_map/all_to_all | solution.py:557
  70.8 5.5 %collective-permute-start.10 = (bf16[24,512]{1,0:T(8,128)(2,1)S(1)}, bf16[24,512]{1,0:T(8,128)(2,1)S(1)}, u32[]{:S(2)}, u32[]{:S(2)}) collective-permute-start(bf16[24,512]{1,0:T(8,128)(2,1)S(1)} %get-tuple-element.77), channel_id=1, source_target_pairs={{0,1},{1,2},{2,3},{3,4},{4,5},{5,6},{6,7},{8,9},{9,10},{10,11},{11... | collective-permute-start | bytes 73736 | tf_op jit(solution)/shard_map/ppermute | solution.py:552
  74.4 5.1 %collective-permute-start.11 = (bf16[24,512]{1,0:T(8,128)(2,1)S(1)}, bf16[24,512]{1,0:T(8,128)(2,1)S(1)}, u32[]{:S(2)}, u32[]{:S(2)}) collective-permute-start(bf16[24,512]{1,0:T(8,128)(2,1)S(1)} %get-tuple-element.78), channel_id=1, source_target_pairs={{1,0},{2,1},{3,2},{4,3},{5,4},{6,5},{7,6},{9,8},{10,9},{11,10},{12... | collective-permute-start | bytes 73736 | tf_op jit(solution)/shard_map/ppermute | solution.py:553
  84.4 4.7 %collective-permute-start.12 = (bf16[4,8,640]{2,1,0:T(8,128)(2,1)S(1)}, bf16[4,8,640]{2,1,0:T(8,128)(2,1)S(1)}, u32[]{:S(2)}, u32[]{:S(2)}) collective-permute-start(bf16[4,8,640]{2,1,0:T(8,128)(2,1)S(1)} %bitcast.24), channel_id=1, source_target_pairs={{0,64},{64,128},{128,192},{192,0},{1,65},{65,129},{129,193},{193,1... | collective-permute-start | bytes 122888 | tf_op jit(solution)/shard_map/ppermute | solution.py:564
  84.5 4.6 %collective-permute-start.13 = (bf16[4,8,640]{2,1,0:T(8,128)(2,1)S(1)}, bf16[4,8,640]{2,1,0:T(8,128)(2,1)S(1)}, u32[]{:S(2)}, u32[]{:S(2)}) collective-permute-start(bf16[4,8,640]{2,1,0:T(8,128)(2,1)S(1)} %bitcast.25), channel_id=1, source_target_pairs={{0,128},{64,192},{128,0},{192,64},{1,129},{65,193},{129,1},{193,65... | collective-permute-start | bytes 122888 | tf_op jit(solution)/shard_map/ppermute | solution.py:564
  85.9 4.0 %collective-permute-start.14 = (bf16[4,8,640]{2,1,0:T(8,128)(2,1)S(1)}, bf16[4,8,640]{2,1,0:T(8,128)(2,1)S(1)}, u32[]{:S(2)}, u32[]{:S(2)}) collective-permute-start(bf16[4,8,640]{2,1,0:T(8,128)(2,1)S(1)} %bitcast.26), channel_id=1, source_target_pairs={{0,192},{64,0},{128,64},{192,128},{1,193},{65,1},{129,65},{193,129... | collective-permute-start | bytes 122888 | tf_op jit(solution)/shard_map/ppermute | solution.py:564
  89.9 48.8 %copy-start.3 = (bf16[512,512]{1,0:T(8,128)(2,1)S(1)}, bf16[512,512]{1,0:T(8,128)(2,1)}, u32[]{:S(2)}) copy-start(bf16[512,512]{1,0:T(8,128)(2,1)} %refs_4_.1) | copy-start | bytes 1572868

commit v2 on v1

--- a/solution.py
+++ b/solution.py
@@ -512,7 +512,6 @@
     signal, pos_idx, live_count, latents, pos_table, w_in, w_kv, w_query, w_out,
     conv_weight, conv_bias, cotangent,
 ):
-    con_dev = signal.shape[0]
     pat_dev = signal.shape[1] // PATCH
     width = w_query.shape[0]
     lat_rows = latents.shape[0]
@@ -522,17 +521,19 @@
     down1 = [(i + 1, i) for i in range(NTM - 1)]
 
     own = make_message(live_count, signal, pos_idx)
-    queries, table, kv_weights, in_weights = prepare(
-        y.reshape(1), z.reshape(1), pos_table, w_kv, w_in, latents, w_query
-    )
+    own, y_one = lax.optimization_barrier((own, y.reshape(1)))
+    below = lax.ppermute(own, "z", shift(NZ, 1))
+    queries, table, kv_weights, in_weights = prepare(y_one, z.reshape(1), pos_table, w_kv, w_in, latents, w_query)
+    own_again, queries = lax.optimization_barrier((own, queries))
 
     def absorbed(messages, state, last=False):
         return absorb(messages, queries, in_weights, kv_weights, table, state, last)
 
-    below, above = own, own
+    above = own_again
     at_hand, state, kvs, valids = [own], None, [], []
     for step in range(1, NZ // 2 + 1):
-        below = lax.ppermute(below, "z", shift(NZ, 1))
+        if step > 1:
+            below = lax.ppermute(below, "z", shift(NZ, 1))
         if step < NZ // 2:
             above = lax.ppermute(above, "z", shift(NZ, -1))
         kv, valid, *state = absorbed(at_hand, state)

time: 140 us -> 140 us (level)
  blocking collectives: 38.4 us -> 36.5 us
    ppermute x4 -> x3, starting transfers between devices: 2.78 us -> 0.17 us  [local(): below = lax.ppermute(below, 'z', shift(NZ, 1))]
    ppermute x3, starting transfers between devices: 9.35 us -> 11.8 us  [local(): above = lax.ppermute(above, 'z', shift(NZ, -1))]
    all_to_all x1, blocking collectives: 23.9 us -> 22.1 us  [local(): dq_all = lax.all_to_all(spread, ('y', 'z', 'tm'), 0, 0, tiled=True)]
  transfers between devices with their start and end apart: 16 -> 16, of which waited for: 6 -> 7; matrix products, arithmetic and copies ran while one was open for 0% -> 0% of each run, Pallas kernels for 24% -> 22%
where the time goes in v2:
time: 140 us
  Pallas kernels  56 us (40%)
  blocking collectives  36.5 us (26%)
  starting transfers between devices  33.3 us (24%)
  waiting for transfers between devices  11.3 us (8%)
  between operations  1.51 us (1%)
    pallas_call x5, Pallas kernels, absorb(): pl.pallas_call(functools.partial(absorb_kernel, fresh=fresh, last=last, c...  36.1 us
    all_to_all x1, blocking collectives, local(): dq_all = lax.all_to_all(spread, ('y', 'z', 'tm'), 0, 0, tiled=True)  22.1 us
    all_to_all x1, blocking collectives, local(): pieces = lax.all_to_all(dq, ('y', 'tm'), 0, 0, tiled=True)  14.5 us
    ppermute x3, starting transfers between devices, local(): above = lax.ppermute(above, 'z', shift(NZ, -1))  11.8 us
    pallas_call x1, Pallas kernels, backward_attention(): pl.pallas_call(functools.partial(backward_kernel, slots=len(msgs)), in_sp...  10.2 us
    all_to_all x1, starting transfers between devices, local(): everyone = lax.all_to_all(copies, 'tm', 0, 0)  8.94 us
    pallas_call x1, Pallas kernels, conv_stack(): pl.pallas_call(conv_kernel, in_specs=[pl.BlockSpec(memory_space=pltpu.SME...  4.83 us
    ppermute x3, waiting for transfers between devices, local(): lax.ppermute(parts[s], 'y', shift(NY, -s))  4.63 us
  transfers between devices with their start and end apart: 16, of which 7 were waited for; matrix products, arithmetic and copies ran while one was open for 0% of the time, Pallas kernels for 22%

profile of v2, /device:TPU:1, one launch (start us, length us, event | category | flops | bytes accessed | tf_op | source)
XLA Modules:
  0.0 140.0 jit_solution(8577802445401948029)
XLA Ops:
  1.3 0.9 make_message.1.refs_0_
  2.2 2.8 %prepare.1 = (bf16[32,512]{1,0:T(8,128)(2,1)S(1)}, bf16[4096,512]{1,0:T(8,128)(2,1)S(1)}, bf16[512,1024]{1,0:T(8,128)(2,1)S(1)}, bf16[32,512]{1,0:T(8,128)(2,1)S(1)}) custom-call(s32[1]{0:T(128)} %bitcast.2.y_ref, s32[1]{0:T(128)} %bitcast.3.z_ref, bf16[4096,512]{1,0:T(8,128)(2,1)} %refs_0_.1, bf16[512,1024]{1,0:T(8,128)(2,1)} %refs_1_.1, ...), custom_call_target="tpu_custom_call" | custom-call | tf_op jit(solution)/shard_map/prepare/pallas_call | solution.py:147
  5.0 6.5 %collective-permute-start.1 = (bf16[256,256]{1,0:T(8,128)(2,1)S(1)}, bf16[256,256]{1,0:T(8,128)(2,1)S(1)}, u32[]{:S(2)}, u32[]{:S(2)}) collective-permute-start(bf16[256,256]{1,0:T(8,128)(2,1)S(1)} %make_message.1.refs_0_), channel_id=1, source_target_pairs={{0,56},{8,0},{16,8},{24,16},{32,24},{40,32},{48,40},{56,48},{1,57}... | collective-permute-start | bytes 393224 | tf_op jit(solution)/shard_map/ppermute | solution.py:538
  11.4 0.0 collective-permute-start
  11.4 4.1 %absorb.5 = (bf16[4,256,1024]{2,1,0:T(8,128)(2,1)}, f32[8,256]{1,0:T(8,128)S(1)}, f32[4,256,512]{2,1,0:T(8,128)S(1)}, f32[4,256,128]{2,1,0:T(8,128)S(1)}) custom-call(bf16[256,256]{1,0:T(8,128)(2,1)S(1)} %make_message.1.refs_0_, bf16[32,512]{1,0:T(8,128)(2,1)S(1)} %get-tuple-element.57.refs_1_.refs_2_.q_ref, ...), custom_call_target="tpu_custom_call" | custom-call | tf_op jit(solution)/shard_map/absorb/pallas_call | solution.py:281
  15.5 0.0 collective-permute-done.1.refs_1_
  15.6 0.9 collective-permute-done.refs_0_
  16.5 0.0 collective-permute-start.2
  16.5 2.7 %collective-permute-start.3 = (bf16[256,256]{1,0:T(8,128)(2,1)S(1)}, bf16[256,256]{1,0:T(8,128)(2,1)S(1)}, u32[]{:S(2)}, u32[]{:S(2)}) collective-permute-start(bf16[256,256]{1,0:T(8,128)(2,1)S(1)} %collective-permute-done.1.refs_1_), channel_id=1, source_target_pairs={{0,56},{8,0},{16,8},{24,16},{32,24},{40,32},{48,40},{56,48},{1,57}... | collective-permute-start | bytes 393224 | tf_op jit(solution)/shard_map/ppermute | solution.py:538
  19.1 8.8 %absorb.6 = (bf16[4,512,1024]{2,1,0:T(8,128)(2,1)}, f32[8,512]{1,0:T(8,128)S(1)}, f32[4,256,512]{2,1,0:T(8,128)S(1)}, f32[4,256,128]{2,1,0:T(8,128)S(1)}) custom-call(bf16[256,256]{1,0:T(8,128)(2,1)S(1)} %collective-permute-done.refs_0_, bf16[256,256]{1,0:T(8,128)(2,1)S(1)} %collective-permute-done.1.refs_1_, ...), custom_call_target="tpu_custom_call", output_to_operand_aliasing={{2}: (6, {}), {3}: (7, {})} | custom-call | tf_op jit(solution)/shard_map/absorb/pallas_call | solution.py:281
  27.9 0.0 collective-permute-done.2.refs_0_
  28.0 0.0 collective-permute-done.3.refs_1_
  28.0 0.1 collective-permute-start.4
  28.1 2.7 %collective-permute-start.5 = (bf16[256,256]{1,0:T(8,128)(2,1)S(1)}, bf16[256,256]{1,0:T(8,128)(2,1)S(1)}, u32[]{:S(2)}, u32[]{:S(2)}) collective-permute-start(bf16[256,256]{1,0:T(8,128)(2,1)S(1)} %collective-permute-done.3.refs_1_), channel_id=1, source_target_pairs={{0,56},{8,0},{16,8},{24,16},{32,24},{40,32},{48,40},{56,48},{1,57}... | collective-permute-start | bytes 393224 | tf_op jit(solution)/shard_map/ppermute | solution.py:538
  30.7 8.8 %absorb.7 = (bf16[4,512,1024]{2,1,0:T(8,128)(2,1)}, f32[8,512]{1,0:T(8,128)S(1)}, f32[4,256,512]{2,1,0:T(8,128)S(1)}, f32[4,256,128]{2,1,0:T(8,128)S(1)}) custom-call(bf16[256,256]{1,0:T(8,128)(2,1)S(1)} %collective-permute-done.2.refs_0_, bf16[256,256]{1,0:T(8,128)(2,1)S(1)} %collective-permute-done.3.refs_1_, ...), custom_call_target="tpu_custom_call", output_to_operand_aliasing={{2}: (6, {}), {3}: (7, {})} | custom-call | tf_op jit(solution)/shard_map/absorb/pallas_call | solution.py:281
  39.5 0.0 collective-permute-done.4.refs_0_
  39.5 0.0 collective-permute-done.5.refs_1_
  39.6 0.1 collective-permute-start.6
  39.6 8.8 %absorb.8 = (bf16[4,512,1024]{2,1,0:T(8,128)(2,1)}, f32[8,512]{1,0:T(8,128)S(1)}, f32[4,256,512]{2,1,0:T(8,128)S(1)}, f32[4,256,128]{2,1,0:T(8,128)S(1)}) custom-call(bf16[256,256]{1,0:T(8,128)(2,1)S(1)} %collective-permute-done.4.refs_0_, bf16[256,256]{1,0:T(8,128)(2,1)S(1)} %collective-permute-done.5.refs_1_, ...), custom_call_target="tpu_custom_call", output_to_operand_aliasing={{2}: (6, {}), {3}: (7, {})} | custom-call | tf_op jit(solution)/shard_map/absorb/pallas_call | solution.py:281
  48.5 0.0 collective-permute-done.6.refs_0_
  48.5 0.0 copy-start.1
  48.5 0.0 copy-start
  48.5 0.0 copy-start.2
  48.5 5.6 %absorb.9 = (bf16[4,256,1024]{2,1,0:T(8,128)(2,1)}, f32[8,256]{1,0:T(8,128)S(1)}, f32[4,8,640]{2,1,0:T(8,128)S(1)}, f32[4,8,640]{2,1,0:T(8,128)S(1)}, f32[4,8,64...) custom-call(bf16[256,256]{1,0:T(8,128)(2,1)S(1)} %collective-permute-done.6.refs_0_, ...), custom_call_target="tpu_custom_call" | custom-call | tf_op jit(solution)/shard_map/absorb/pallas_call | solution.py:281
  54.1 2.8 %collective-permute-start.7 = (f32[4,8,640]{2,1,0:T(8,128)S(1)}, f32[4,8,640]{2,1,0:T(8,128)S(1)}, u32[]{:S(2)}, u32[]{:S(2)}) collective-permute-start(f32[4,8,640]{2,1,0:T(8,128)S(1)} %get-tuple-element.79), channel_id=1, source_target_pairs={{0,192},{64,0},{128,64},{192,128},{1,193},{65,1},{129,65},{193,129... | collective-permute-start | bytes 245768 | tf_op jit(solution)/shard_map/ppermute | solution.py:549
  57.0 0.5 collective-permute-start.8
  57.5 0.5 collective-permute-start.9
  58.0 0.4 collective-permute-done.7.refs_1_
  58.5 3.4 %collective-permute-done.8.refs_2_ = f32[4,8,640]{2,1,0:T(8,128)S(1)} collective-permute-done((f32[4,8,640]{2,1,0:T(8,128)S(1)}, f32[4,8,640]{2,1,0:T(8,128)S(1)}, u32[]{:S(2)}, u32[]{:S(2)}) %collective-permute-start.8) | collective-permute-done | bytes 81952 | tf_op jit(solution)/shard_map/ppermute | solution.py:549
  61.8 0.8 collective-permute-done.9.refs_3_
  62.6 1.1 combine_parts.1
  63.8 8.9 %all-to-all-start = ((bf16[8,32,512]{2,1,0:T(8,128)(2,1)}), bf16[8,32,512]{2,1,0:T(8,128)(2,1)S(1)}, u32[]{:S(2)}, u32[]{:S(2)}) async-start(bf16[8,32,512]{2,1,0:T(8,128)(2,1)} %get-tuple-element.83), calls=%async_computation | async-start | bytes 524288 | tf_op jit(solution)/shard_map/all_to_all | solution.py:558
  72.7 0.0 copy-done.1
  72.7 3.5 %collective-permute-start.10 = (bf16[24,512]{1,0:T(8,128)(2,1)S(1)}, bf16[24,512]{1,0:T(8,128)(2,1)S(1)}, u32[]{:S(2)}, u32[]{:S(2)}) collective-permute-start(bf16[24,512]{1,0:T(8,128)(2,1)S(1)} %get-tuple-element.85), channel_id=1, source_target_pairs={{0,1},{1,2},{2,3},{3,4},{4,5},{5,6},{6,7},{8,9},{9,10},{10,11},{11... | collective-permute-start | bytes 73736 | tf_op jit(solution)/shard_map/ppermute | solution.py:553
  76.3 1.9 %collective-permute-start.11 = (bf16[24,512]{1,0:T(8,128)(2,1)S(1)}, bf16[24,512]{1,0:T(8,128)(2,1)S(1)}, u32[]{:S(2)}, u32[]{:S(2)}) collective-permute-start(bf16[24,512]{1,0:T(8,128)(2,1)S(1)} %get-tuple-element.86), channel_id=1, source_target_pairs={{1,0},{2,1},{3,2},{4,3},{5,4},{6,5},{7,6},{9,8},{10,9},{11,10},{12... | collective-permute-start | bytes 73736 | tf_op jit(solution)/shard_map/ppermute | solution.py:554
  78.2 0.0 collective-permute-done.10.cl_ref
  78.2 3.2 %collective-permute-done.11.cr_ref = bf16[24,512]{1,0:T(8,128)(2,1)S(1)} collective-permute-done((bf16[24,512]{1,0:T(8,128)(2,1)S(1)}, bf16[24,512]{1,0:T(8,128)(2,1)S(1)}, u32[]{:S(2)}, u32[]{:S(2)}) %collective-permute-start.11) | collective-permute-done | bytes 24608 | tf_op jit(solution)/shard_map/ppermute | solution.py:554
  81.4 0.0 all-to-all-done
  81.4 0.0 copy-done
  81.4 0.0 copy-done.2
  81.4 4.8 %conv_stack.1 = (bf16[32,512]{1,0:T(8,128)(2,1)}, bf16[32,640]{1,0:T(8,128)(2,1)S(1)}, bf16[256,1024]{1,0:T(8,128)(2,1)S(1)}, bf16[512,1024]{1,0:T(8,128)(2,1)S(...) custom-call(s32[1]{0:T(128)} %bitcast.tm_ref, ...), custom_call_target="tpu_custom_call" | custom-call | tf_op jit(solution)/shard_map/conv_stack/pallas_call | solution.py:414
  86.3 0.1 collective-permute-start.12
  86.4 1.5 %collective-permute-start.13 = (bf16[4,8,640]{2,1,0:T(8,128)(2,1)S(1)}, bf16[4,8,640]{2,1,0:T(8,128)(2,1)S(1)}, u32[]{:S(2)}, u32[]{:S(2)}) collective-permute-start(bf16[4,8,640]{2,1,0:T(8,128)(2,1)S(1)} %bitcast.25), channel_id=1, source_target_pairs={{0,128},{64,192},{128,0},{192,64},{1,129},{65,193},{129,1},{193,65... | collective-permute-start | bytes 122888 | tf_op jit(solution)/shard_map/ppermute | solution.py:565
  87.8 1.5 %collective-permute-start.14 = (bf16[4,8,640]{2,1,0:T(8,128)(2,1)S(1)}, bf16[4,8,640]{2,1,0:T(8,128)(2,1)S(1)}, u32[]{:S(2)}, u32[]{:S(2)}) collective-permute-start(bf16[4,8,640]{2,1,0:T(8,128)(2,1)S(1)} %bitcast.26), channel_id=1, source_target_pairs={{0,192},{64,0},{128,64},{192,128},{1,193},{65,1},{129,65},{193,129... | collective-permute-start | bytes 122888 | tf_op jit(solution)/shard_map/ppermute | solution.py:565
  89.3 1.7 %collective-permute-done.12.refs_1_ = bf16[4,8,640]{2,1,0:T(8,128)(2,1)S(1)} collective-permute-done((bf16[4,8,640]{2,1,0:T(8,128)(2,1)S(1)}, bf16[4,8,640]{2,1,0:T(8,128)(2,1)S(1)}, u32[]{:S(2)}, u32[]{:S(2)}) %collective-permute-start.12) | collective-permute-done | bytes 40992 | tf_op jit(solution)/shard_map/ppermute | solution.py:565
  91.0 0.0 collective-permute-done.13.refs_2_
  91.0 0.9 collective-permute-done.14.refs_3_
  91.8 0.0 copy-start.3
  91.8 10.2 %backward_attention.1 = f32[32,512]{1,0:T(8,128)S(1)} custom-call(s32[1]{0:T(128)} %bitcast.2.y_ref, bf16[32,512]{1,0:T(8,128)(2,1)S(1)} %get-tuple-element.57.refs_1_.refs_2_.q_ref, bf16[4,8,640]{2,1,0:T(8,128)(2,1)S(1)} %bitcast.27, bf16[4,8,640]{2,1,0:T(8,128)(2,1)S(1)} %collective-permute-done.12.refs_1_, ...), custom_call_target="tpu_custom_call" | custom-call | tf_op jit(solution)/shard_map/backward_attention/pallas_call | solution.py:492
  102.1 0.1 copy.20
  102.1 14.5 %all_to_all.19 = f32[32,1,512]{2,1,0:T(1,128)S(1)} all-to-all(f32[32,1,512]{2,1,0:T(1,128)S(1)} %copy.20), channel_id=1, replica_groups=mesh['y'=4,'z'=8,'tm'=8] {'y','tm'}, dimensions={0} | all-to-all | bytes 131072 | tf_op jit(solution)/shard_map/all_to_all | solution.py:568
  116.6 0.1 reduce_sum.9
  116.7 0.1 broadcast_in_dim.2
  116.7 22.1 %all_to_all.20 = bf16[256,4,128]{2,1,0:T(4,128)(2,1)S(1)} all-to-all(bf16[256,4,128]{2,1,0:T(4,128)(2,1)S(1)} %broadcast_in_dim.2), channel_id=1, replica_groups=mesh['y'=4,'z'=8,'tm'=8] {'y','z','tm'}, dimensions={0} | all-to-all | bytes 524288 | tf_op jit(solution)/shard_map/all_to_all | solution.py:571
  138.8 0.0 copy-done.3
  138.8 1.1 fusion
  (1 shorter events, 0.0 us)
Async XLA Ops:
  5.0 10.6 %collective-permute-start.1 = (bf16[256,256]{1,0:T(8,128)(2,1)S(1)}, bf16[256,256]{1,0:T(8,128)(2,1)S(1)}, u32[]{:S(2)}, u32[]{:S(2)}) collective-permute-start(bf16[256,256]{1,0:T(8,128)(2,1)S(1)} %make_message.1.refs_0_), channel_id=1, source_target_pairs={{0,56},{8,0},{16,8},{24,16},{32,24},{40,32},{48,40},{56,48},{1,57}... | collective-permute-start | bytes 393224 | tf_op jit(solution)/shard_map/ppermute | solution.py:538
  11.4 5.0 %collective-permute-start = (bf16[256,256]{1,0:T(8,128)(2,1)S(1)}, bf16[256,256]{1,0:T(8,128)(2,1)S(1)}, u32[]{:S(2)}, u32[]{:S(2)}) collective-permute-start(bf16[256,256]{1,0:T(8,128)(2,1)S(1)} %make_message.1.refs_0_), channel_id=1, source_target_pairs={{0,8},{8,16},{16,24},{24,32},{32,40},{40,48},{48,56},{56,0},{1,9},... | collective-permute-start | bytes 393224 | tf_op jit(solution)/shard_map/ppermute | solution.py:525
  16.5 11.5 %collective-permute-start.2 = (bf16[256,256]{1,0:T(8,128)(2,1)S(1)}, bf16[256,256]{1,0:T(8,128)(2,1)S(1)}, u32[]{:S(2)}, u32[]{:S(2)}) collective-permute-start(bf16[256,256]{1,0:T(8,128)(2,1)S(1)} %collective-permute-done.refs_0_), channel_id=1, source_target_pairs={{0,8},{8,16},{16,24},{24,32},{32,40},{40,48},{48,56},{56,0},{1,9},... | collective-permute-start | bytes 393224 | tf_op jit(solution)/shard_map/ppermute | solution.py:536
  16.5 11.5 %collective-permute-start.3 = (bf16[256,256]{1,0:T(8,128)(2,1)S(1)}, bf16[256,256]{1,0:T(8,128)(2,1)S(1)}, u32[]{:S(2)}, u32[]{:S(2)}) collective-permute-start(bf16[256,256]{1,0:T(8,128)(2,1)S(1)} %collective-permute-done.1.refs_1_), channel_id=1, source_target_pairs={{0,56},{8,0},{16,8},{24,16},{32,24},{40,32},{48,40},{56,48},{1,57}... | collective-permute-start | bytes 393224 | tf_op jit(solution)/shard_map/ppermute | solution.py:538
  28.0 11.6 %collective-permute-start.4 = (bf16[256,256]{1,0:T(8,128)(2,1)S(1)}, bf16[256,256]{1,0:T(8,128)(2,1)S(1)}, u32[]{:S(2)}, u32[]{:S(2)}) collective-permute-start(bf16[256,256]{1,0:T(8,128)(2,1)S(1)} %collective-permute-done.2.refs_0_), channel_id=1, source_target_pairs={{0,8},{8,16},{16,24},{24,32},{32,40},{40,48},{48,56},{56,0},{1,9},... | collective-permute-start | bytes 393224 | tf_op jit(solution)/shard_map/ppermute | solution.py:536
  28.1 11.5 %collective-permute-start.5 = (bf16[256,256]{1,0:T(8,128)(2,1)S(1)}, bf16[256,256]{1,0:T(8,128)(2,1)S(1)}, u32[]{:S(2)}, u32[]{:S(2)}) collective-permute-start(bf16[256,256]{1,0:T(8,128)(2,1)S(1)} %collective-permute-done.3.refs_1_), channel_id=1, source_target_pairs={{0,56},{8,0},{16,8},{24,16},{32,24},{40,32},{48,40},{56,48},{1,57}... | collective-permute-start | bytes 393224 | tf_op jit(solution)/shard_map/ppermute | solution.py:538
  39.6 8.9 %collective-permute-start.6 = (bf16[256,256]{1,0:T(8,128)(2,1)S(1)}, bf16[256,256]{1,0:T(8,128)(2,1)S(1)}, u32[]{:S(2)}, u32[]{:S(2)}) collective-permute-start(bf16[256,256]{1,0:T(8,128)(2,1)S(1)} %collective-permute-done.4.refs_0_), channel_id=1, source_target_pairs={{0,8},{8,16},{16,24},{24,32},{32,40},{40,48},{48,56},{56,0},{1,9},... | collective-permute-start | bytes 393224 | tf_op jit(solution)/shard_map/ppermute | solution.py:536
  48.5 24.2 %copy-start.1 = (bf16[4,8,512]{2,1,0:T(8,128)(2,1)S(1)}, bf16[4,8,512]{2,1,0:T(8,128)(2,1)}, u32[]{:S(2)}) copy-start(bf16[4,8,512]{2,1,0:T(8,128)(2,1)} %param.23) | copy-start | bytes 98308
  48.5 32.9 %copy-start = (bf16[512,512]{1,0:T(8,128)(2,1)S(1)}, bf16[512,512]{1,0:T(8,128)(2,1)}, u32[]{:S(2)}) copy-start(bf16[512,512]{1,0:T(8,128)(2,1)} %w_out_ref.1) | copy-start | bytes 1572868
  48.5 32.9 %copy-start.2 = (f32[2,512]{1,0:T(2,128)S(1)}, f32[2,512]{1,0:T(2,128)}, u32[]{:S(2)}) copy-start(f32[2,512]{1,0:T(2,128)} %bias_ref.1) | copy-start | bytes 12292
  54.1 4.3 %collective-permute-start.7 = (f32[4,8,640]{2,1,0:T(8,128)S(1)}, f32[4,8,640]{2,1,0:T(8,128)S(1)}, u32[]{:S(2)}, u32[]{:S(2)}) collective-permute-start(f32[4,8,640]{2,1,0:T(8,128)S(1)} %get-tuple-element.79), channel_id=1, source_target_pairs={{0,192},{64,0},{128,64},{192,128},{1,193},{65,1},{129,65},{193,129... | collective-permute-start | bytes 245768 | tf_op jit(solution)/shard_map/ppermute | solution.py:549
  57.0 4.9 %collective-permute-start.8 = (f32[4,8,640]{2,1,0:T(8,128)S(1)}, f32[4,8,640]{2,1,0:T(8,128)S(1)}, u32[]{:S(2)}, u32[]{:S(2)}) collective-permute-start(f32[4,8,640]{2,1,0:T(8,128)S(1)} %get-tuple-element.80), channel_id=1, source_target_pairs={{0,128},{64,192},{128,0},{192,64},{1,129},{65,193},{129,1},{193,65... | collective-permute-start | bytes 245768 | tf_op jit(solution)/shard_map/ppermute | solution.py:549
  57.5 5.2 %collective-permute-start.9 = (f32[4,8,640]{2,1,0:T(8,128)S(1)}, f32[4,8,640]{2,1,0:T(8,128)S(1)}, u32[]{:S(2)}, u32[]{:S(2)}) collective-permute-start(f32[4,8,640]{2,1,0:T(8,128)S(1)} %get-tuple-element.81), channel_id=1, source_target_pairs={{0,64},{64,128},{128,192},{192,0},{1,65},{65,129},{129,193},{193,1... | collective-permute-start | bytes 245768 | tf_op jit(solution)/shard_map/ppermute | solution.py:549
  63.8 17.6 %all-to-all-start = ((bf16[8,32,512]{2,1,0:T(8,128)(2,1)}), bf16[8,32,512]{2,1,0:T(8,128)(2,1)S(1)}, u32[]{:S(2)}, u32[]{:S(2)}) async-start(bf16[8,32,512]{2,1,0:T(8,128)(2,1)} %get-tuple-element.83), calls=%async_computation | async-start | bytes 524288 | tf_op jit(solution)/shard_map/all_to_all | solution.py:558
  72.7 5.5 %collective-permute-start.10 = (bf16[24,512]{1,0:T(8,128)(2,1)S(1)}, bf16[24,512]{1,0:T(8,128)(2,1)S(1)}, u32[]{:S(2)}, u32[]{:S(2)}) collective-permute-start(bf16[24,512]{1,0:T(8,128)(2,1)S(1)} %get-tuple-element.85), channel_id=1, source_target_pairs={{0,1},{1,2},{2,3},{3,4},{4,5},{5,6},{6,7},{8,9},{9,10},{10,11},{11... | collective-permute-start | bytes 73736 | tf_op jit(solution)/shard_map/ppermute | solution.py:553
  76.3 5.1 %collective-permute-start.11 = (bf16[24,512]{1,0:T(8,128)(2,1)S(1)}, bf16[24,512]{1,0:T(8,128)(2,1)S(1)}, u32[]{:S(2)}, u32[]{:S(2)}) collective-permute-start(bf16[24,512]{1,0:T(8,128)(2,1)S(1)} %get-tuple-element.86), channel_id=1, source_target_pairs={{1,0},{2,1},{3,2},{4,3},{5,4},{6,5},{7,6},{9,8},{10,9},{11,10},{12... | collective-permute-start | bytes 73736 | tf_op jit(solution)/shard_map/ppermute | solution.py:554
  86.3 4.7 %collective-permute-start.12 = (bf16[4,8,640]{2,1,0:T(8,128)(2,1)S(1)}, bf16[4,8,640]{2,1,0:T(8,128)(2,1)S(1)}, u32[]{:S(2)}, u32[]{:S(2)}) collective-permute-start(bf16[4,8,640]{2,1,0:T(8,128)(2,1)S(1)} %bitcast.24), channel_id=1, source_target_pairs={{0,64},{64,128},{128,192},{192,0},{1,65},{65,129},{129,193},{193,1... | collective-permute-start | bytes 122888 | tf_op jit(solution)/shard_map/ppermute | solution.py:565
  86.4 4.6 %collective-permute-start.13 = (bf16[4,8,640]{2,1,0:T(8,128)(2,1)S(1)}, bf16[4,8,640]{2,1,0:T(8,128)(2,1)S(1)}, u32[]{:S(2)}, u32[]{:S(2)}) collective-permute-start(bf16[4,8,640]{2,1,0:T(8,128)(2,1)S(1)} %bitcast.25), channel_id=1, source_target_pairs={{0,128},{64,192},{128,0},{192,64},{1,129},{65,193},{129,1},{193,65... | collective-permute-start | bytes 122888 | tf_op jit(solution)/shard_map/ppermute | solution.py:565
  87.8 4.0 %collective-permute-start.14 = (bf16[4,8,640]{2,1,0:T(8,128)(2,1)S(1)}, bf16[4,8,640]{2,1,0:T(8,128)(2,1)S(1)}, u32[]{:S(2)}, u32[]{:S(2)}) collective-permute-start(bf16[4,8,640]{2,1,0:T(8,128)(2,1)S(1)} %bitcast.26), channel_id=1, source_target_pairs={{0,192},{64,0},{128,64},{192,128},{1,193},{65,1},{129,65},{193,129... | collective-permute-start | bytes 122888 | tf_op jit(solution)/shard_map/ppermute | solution.py:565
  91.8 47.0 %copy-start.3 = (bf16[512,512]{1,0:T(8,128)(2,1)S(1)}, bf16[512,512]{1,0:T(8,128)(2,1)}, u32[]{:S(2)}) copy-start(bf16[512,512]{1,0:T(8,128)(2,1)} %refs_4_.1) | copy-start | bytes 1572868

commit v3 on v1

--- a/solution.py
+++ b/solution.py
@@ -21,7 +21,7 @@
 
 NY, NZ, NTM = 4, 8, 8
 MIB = 1 << 20
-PIECE, PARTS, HALVES, VMEM_ABSORB = 2048, 2, 2, 28
+PIECE, PARTS, HALVES, VMEM_ABSORB = 4096, 2, 2, 28
 WUNROLL, VMEM_BACK = 4, 40
 
 
@@ -185,14 +185,8 @@
     valid_ref[...] = jnp.broadcast_to(valid, valid_ref.shape)
     piece = PIECE
     ids = lax.broadcasted_iota(jnp.int32, (rows, piece), 1).astype(f32)
-    pos_ref[...] = jnp.zeros_like(pos_ref)
-
-    @pl.loop(0, table_ref.shape[0] // piece)
-    def _(k):
-        start = pl.multiple_of(k * piece, piece)
-        hot = jnp.where(ids == idx - start.astype(f32), 1.0, 0.0).astype(bf16)
-        pos_ref[...] = pos_ref[...] + nn_dot(hot, table_ref[pl.ds(start, piece), :])
-
+    hot = jnp.where(ids == idx, 1.0, 0.0).astype(bf16)
+    pos_ref[...] = nn_dot(hot, table_ref[...])
     tall = jnp.concatenate([w_in_ref[...]] * windows, axis=0)
     band = lax.broadcasted_iota(jnp.int32, sig.shape, 1) // PATCH
     for w in range(windows):

time: 140 us -> 138 us (0.986)
  Pallas kernels: 56 us -> 53.5 us
    pallas_call x5, Pallas kernels: 36.1 us -> 33.6 us  [absorb(): pl.pallas_call(functools.partial(absorb_kernel, fresh=fresh, last=last, c...]
  transfers between devices with their start and end apart: 16 -> 16, of which waited for: 6 -> 6; matrix products, arithmetic and copies ran while one was open for 0% -> 0% of each run, Pallas kernels for 24% -> 23%
where the time goes in v3:
time: 138 us
  Pallas kernels  53.5 us (39%)
  blocking collectives  38.4 us (28%)
  starting transfers between devices  32.5 us (24%)
  waiting for transfers between devices  10.4 us (8%)
  between operations  1.52 us (1%)
    pallas_call x5, Pallas kernels, absorb(): pl.pallas_call(functools.partial(absorb_kernel, fresh=fresh, last=last, c...  33.6 us
    all_to_all x1, blocking collectives, local(): dq_all = lax.all_to_all(spread, ('y', 'z', 'tm'), 0, 0, tiled=True)  23.9 us
    all_to_all x1, blocking collectives, local(): pieces = lax.all_to_all(dq, ('y', 'tm'), 0, 0, tiled=True)  14.5 us
    pallas_call x1, Pallas kernels, backward_attention(): pl.pallas_call(functools.partial(backward_kernel, slots=len(msgs)), in_sp...  10.2 us
    ppermute x3, starting transfers between devices, local(): above = lax.ppermute(above, 'z', shift(NZ, -1))  9.35 us
    all_to_all x1, starting transfers between devices, local(): everyone = lax.all_to_all(copies, 'tm', 0, 0)  7.8 us
    pallas_call x1, Pallas kernels, conv_stack(): pl.pallas_call(conv_kernel, in_specs=[pl.BlockSpec(memory_space=pltpu.SME...  4.83 us
    ppermute x3, waiting for transfers between devices, local(): lax.ppermute(parts[s], 'y', shift(NY, -s))  4.63 us
  transfers between devices with their start and end apart: 16, of which 6 were waited for; matrix products, arithmetic and copies ran while one was open for 0% of the time, Pallas kernels for 23%

profile of v3, /device:TPU:1, one launch (start us, length us, event | category | flops | bytes accessed | tf_op | source)
XLA Modules:
  0.0 137.7 jit_solution(11130616920534405984)
XLA Ops:
  1.3 0.9 make_message.1.refs_0_
  2.2 2.5 %collective-permute-start = (bf16[256,256]{1,0:T(8,128)(2,1)S(1)}, bf16[256,256]{1,0:T(8,128)(2,1)S(1)}, u32[]{:S(2)}, u32[]{:S(2)}) collective-permute-start(bf16[256,256]{1,0:T(8,128)(2,1)S(1)} %make_message.1.refs_0_), channel_id=1, source_target_pairs={{0,8},{8,16},{16,24},{24,32},{32,40},{40,48},{48,56},{56,0},{1,9},... | collective-permute-start | bytes 393224 | tf_op jit(solution)/shard_map/ppermute | solution.py:529
  4.7 4.0 %collective-permute-start.1 = (bf16[256,256]{1,0:T(8,128)(2,1)S(1)}, bf16[256,256]{1,0:T(8,128)(2,1)S(1)}, u32[]{:S(2)}, u32[]{:S(2)}) collective-permute-start(bf16[256,256]{1,0:T(8,128)(2,1)S(1)} %make_message.1.refs_0_), channel_id=1, source_target_pairs={{0,56},{8,0},{16,8},{24,16},{32,24},{40,32},{48,40},{56,48},{1,57}... | collective-permute-start | bytes 393224 | tf_op jit(solution)/shard_map/ppermute | solution.py:531
  8.7 2.8 %prepare.1 = (bf16[32,512]{1,0:T(8,128)(2,1)S(1)}, bf16[4096,512]{1,0:T(8,128)(2,1)S(1)}, bf16[512,1024]{1,0:T(8,128)(2,1)S(1)}, bf16[32,512]{1,0:T(8,128)(2,1)S(1)}) custom-call(s32[1]{0:T(128)} %bitcast.2.y_ref, s32[1]{0:T(128)} %bitcast.3.z_ref, bf16[4096,512]{1,0:T(8,128)(2,1)} %refs_0_.1, bf16[512,1024]{1,0:T(8,128)(2,1)} %refs_1_.1, ...), custom_call_target="tpu_custom_call" | custom-call | tf_op jit(solution)/shard_map/prepare/pallas_call | solution.py:147
  11.5 3.8 %absorb.5 = (bf16[4,256,1024]{2,1,0:T(8,128)(2,1)}, f32[8,256]{1,0:T(8,128)S(1)}, f32[4,256,512]{2,1,0:T(8,128)S(1)}, f32[4,256,128]{2,1,0:T(8,128)S(1)}) custom-call(bf16[256,256]{1,0:T(8,128)(2,1)S(1)} %make_message.1.refs_0_, bf16[32,512]{1,0:T(8,128)(2,1)S(1)} %get-tuple-element.49.refs_1_.refs_2_.q_ref, ...), custom_call_target="tpu_custom_call" | custom-call | tf_op jit(solution)/shard_map/absorb/pallas_call | solution.py:275
  15.3 0.0 collective-permute-done.refs_0_
  15.3 0.0 collective-permute-done.1.refs_1_
  15.3 0.1 collective-permute-start.2
  15.4 2.7 %collective-permute-start.3 = (bf16[256,256]{1,0:T(8,128)(2,1)S(1)}, bf16[256,256]{1,0:T(8,128)(2,1)S(1)}, u32[]{:S(2)}, u32[]{:S(2)}) collective-permute-start(bf16[256,256]{1,0:T(8,128)(2,1)S(1)} %collective-permute-done.1.refs_1_), channel_id=1, source_target_pairs={{0,56},{8,0},{16,8},{24,16},{32,24},{40,32},{48,40},{56,48},{1,57}... | collective-permute-start | bytes 393224 | tf_op jit(solution)/shard_map/ppermute | solution.py:531
  18.1 8.4 %absorb.6 = (bf16[4,512,1024]{2,1,0:T(8,128)(2,1)}, f32[8,512]{1,0:T(8,128)S(1)}, f32[4,256,512]{2,1,0:T(8,128)S(1)}, f32[4,256,128]{2,1,0:T(8,128)S(1)}) custom-call(bf16[256,256]{1,0:T(8,128)(2,1)S(1)} %collective-permute-done.refs_0_, bf16[256,256]{1,0:T(8,128)(2,1)S(1)} %collective-permute-done.1.refs_1_, ...), custom_call_target="tpu_custom_call", output_to_operand_aliasing={{2}: (6, {}), {3}: (7, {})} | custom-call | tf_op jit(solution)/shard_map/absorb/pallas_call | solution.py:275
  26.5 0.0 collective-permute-done.2.refs_0_
  26.5 0.0 collective-permute-done.3.refs_1_
  26.5 0.1 collective-permute-start.4
  26.6 2.7 %collective-permute-start.5 = (bf16[256,256]{1,0:T(8,128)(2,1)S(1)}, bf16[256,256]{1,0:T(8,128)(2,1)S(1)}, u32[]{:S(2)}, u32[]{:S(2)}) collective-permute-start(bf16[256,256]{1,0:T(8,128)(2,1)S(1)} %collective-permute-done.3.refs_1_), channel_id=1, source_target_pairs={{0,56},{8,0},{16,8},{24,16},{32,24},{40,32},{48,40},{56,48},{1,57}... | collective-permute-start | bytes 393224 | tf_op jit(solution)/shard_map/ppermute | solution.py:531
  29.3 8.4 %absorb.7 = (bf16[4,512,1024]{2,1,0:T(8,128)(2,1)}, f32[8,512]{1,0:T(8,128)S(1)}, f32[4,256,512]{2,1,0:T(8,128)S(1)}, f32[4,256,128]{2,1,0:T(8,128)S(1)}) custom-call(bf16[256,256]{1,0:T(8,128)(2,1)S(1)} %collective-permute-done.2.refs_0_, bf16[256,256]{1,0:T(8,128)(2,1)S(1)} %collective-permute-done.3.refs_1_, ...), custom_call_target="tpu_custom_call", output_to_operand_aliasing={{2}: (6, {}), {3}: (7, {})} | custom-call | tf_op jit(solution)/shard_map/absorb/pallas_call | solution.py:275
  37.7 0.0 collective-permute-done.4.refs_0_
  37.7 0.0 collective-permute-done.5.refs_1_
  37.7 0.1 collective-permute-start.6
  37.8 8.4 %absorb.8 = (bf16[4,512,1024]{2,1,0:T(8,128)(2,1)}, f32[8,512]{1,0:T(8,128)S(1)}, f32[4,256,512]{2,1,0:T(8,128)S(1)}, f32[4,256,128]{2,1,0:T(8,128)S(1)}) custom-call(bf16[256,256]{1,0:T(8,128)(2,1)S(1)} %collective-permute-done.4.refs_0_, bf16[256,256]{1,0:T(8,128)(2,1)S(1)} %collective-permute-done.5.refs_1_, ...), custom_call_target="tpu_custom_call", output_to_operand_aliasing={{2}: (6, {}), {3}: (7, {})} | custom-call | tf_op jit(solution)/shard_map/absorb/pallas_call | solution.py:275
  46.3 0.0 collective-permute-done.6.refs_0_
  46.3 0.0 copy-start.1
  46.3 0.0 copy-start
  46.3 0.0 copy-start.2
  46.3 4.6 %absorb.9 = (bf16[4,256,1024]{2,1,0:T(8,128)(2,1)}, f32[8,256]{1,0:T(8,128)S(1)}, f32[4,8,640]{2,1,0:T(8,128)S(1)}, f32[4,8,640]{2,1,0:T(8,128)S(1)}, f32[4,8,64...) custom-call(bf16[256,256]{1,0:T(8,128)(2,1)S(1)} %collective-permute-done.6.refs_0_, ...), custom_call_target="tpu_custom_call" | custom-call | tf_op jit(solution)/shard_map/absorb/pallas_call | solution.py:275
  50.9 3.0 %collective-permute-start.7 = (f32[4,8,640]{2,1,0:T(8,128)S(1)}, f32[4,8,640]{2,1,0:T(8,128)S(1)}, u32[]{:S(2)}, u32[]{:S(2)}) collective-permute-start(f32[4,8,640]{2,1,0:T(8,128)S(1)} %get-tuple-element.71), channel_id=1, source_target_pairs={{0,192},{64,0},{128,64},{192,128},{1,193},{65,1},{129,65},{193,129... | collective-permute-start | bytes 245768 | tf_op jit(solution)/shard_map/ppermute | solution.py:542
  53.9 0.4 collective-permute-start.8
  54.3 0.7 collective-permute-start.9
  55.0 0.4 collective-permute-done.7.refs_1_
  55.4 3.4 %collective-permute-done.8.refs_2_ = f32[4,8,640]{2,1,0:T(8,128)S(1)} collective-permute-done((f32[4,8,640]{2,1,0:T(8,128)S(1)}, f32[4,8,640]{2,1,0:T(8,128)S(1)}, u32[]{:S(2)}, u32[]{:S(2)}) %collective-permute-start.8) | collective-permute-done | bytes 81952 | tf_op jit(solution)/shard_map/ppermute | solution.py:542
  58.8 0.8 collective-permute-done.9.refs_3_
  59.6 1.1 combine_parts.1
  60.7 7.8 %all-to-all-start = ((bf16[8,32,512]{2,1,0:T(8,128)(2,1)}), bf16[8,32,512]{2,1,0:T(8,128)(2,1)S(1)}, u32[]{:S(2)}, u32[]{:S(2)}) async-start(bf16[8,32,512]{2,1,0:T(8,128)(2,1)} %get-tuple-element.75), calls=%async_computation | async-start | bytes 524288 | tf_op jit(solution)/shard_map/all_to_all | solution.py:551
  68.5 0.0 copy-done.1
  68.5 3.5 %collective-permute-start.10 = (bf16[24,512]{1,0:T(8,128)(2,1)S(1)}, bf16[24,512]{1,0:T(8,128)(2,1)S(1)}, u32[]{:S(2)}, u32[]{:S(2)}) collective-permute-start(bf16[24,512]{1,0:T(8,128)(2,1)S(1)} %get-tuple-element.77), channel_id=1, source_target_pairs={{0,1},{1,2},{2,3},{3,4},{4,5},{5,6},{6,7},{8,9},{9,10},{10,11},{11... | collective-permute-start | bytes 73736 | tf_op jit(solution)/shard_map/ppermute | solution.py:546
  72.1 1.9 %collective-permute-start.11 = (bf16[24,512]{1,0:T(8,128)(2,1)S(1)}, bf16[24,512]{1,0:T(8,128)(2,1)S(1)}, u32[]{:S(2)}, u32[]{:S(2)}) collective-permute-start(bf16[24,512]{1,0:T(8,128)(2,1)S(1)} %get-tuple-element.78), channel_id=1, source_target_pairs={{1,0},{2,1},{3,2},{4,3},{5,4},{6,5},{7,6},{9,8},{10,9},{11,10},{12... | collective-permute-start | bytes 73736 | tf_op jit(solution)/shard_map/ppermute | solution.py:547
  74.0 0.0 collective-permute-done.10.cl_ref
  74.0 3.2 %collective-permute-done.11.cr_ref = bf16[24,512]{1,0:T(8,128)(2,1)S(1)} collective-permute-done((bf16[24,512]{1,0:T(8,128)(2,1)S(1)}, bf16[24,512]{1,0:T(8,128)(2,1)S(1)}, u32[]{:S(2)}, u32[]{:S(2)}) %collective-permute-start.11) | collective-permute-done | bytes 24608 | tf_op jit(solution)/shard_map/ppermute | solution.py:547
  77.2 0.0 all-to-all-done
  77.2 0.0 copy-done
  77.2 0.0 copy-done.2
  77.2 4.8 %conv_stack.1 = (bf16[32,512]{1,0:T(8,128)(2,1)}, bf16[32,640]{1,0:T(8,128)(2,1)S(1)}, bf16[256,1024]{1,0:T(8,128)(2,1)S(1)}, bf16[512,1024]{1,0:T(8,128)(2,1)S(...) custom-call(s32[1]{0:T(128)} %bitcast.tm_ref, ...), custom_call_target="tpu_custom_call" | custom-call | tf_op jit(solution)/shard_map/conv_stack/pallas_call | solution.py:408
  82.1 0.1 collective-permute-start.12
  82.2 1.5 %collective-permute-start.13 = (bf16[4,8,640]{2,1,0:T(8,128)(2,1)S(1)}, bf16[4,8,640]{2,1,0:T(8,128)(2,1)S(1)}, u32[]{:S(2)}, u32[]{:S(2)}) collective-permute-start(bf16[4,8,640]{2,1,0:T(8,128)(2,1)S(1)} %bitcast.25), channel_id=1, source_target_pairs={{0,128},{64,192},{128,0},{192,64},{1,129},{65,193},{129,1},{193,65... | collective-permute-start | bytes 122888 | tf_op jit(solution)/shard_map/ppermute | solution.py:558
  83.6 1.5 %collective-permute-start.14 = (bf16[4,8,640]{2,1,0:T(8,128)(2,1)S(1)}, bf16[4,8,640]{2,1,0:T(8,128)(2,1)S(1)}, u32[]{:S(2)}, u32[]{:S(2)}) collective-permute-start(bf16[4,8,640]{2,1,0:T(8,128)(2,1)S(1)} %bitcast.26), channel_id=1, source_target_pairs={{0,192},{64,0},{128,64},{192,128},{1,193},{65,1},{129,65},{193,129... | collective-permute-start | bytes 122888 | tf_op jit(solution)/shard_map/ppermute | solution.py:558
  85.1 1.7 %collective-permute-done.12.refs_1_ = bf16[4,8,640]{2,1,0:T(8,128)(2,1)S(1)} collective-permute-done((bf16[4,8,640]{2,1,0:T(8,128)(2,1)S(1)}, bf16[4,8,640]{2,1,0:T(8,128)(2,1)S(1)}, u32[]{:S(2)}, u32[]{:S(2)}) %collective-permute-start.12) | collective-permute-done | bytes 40992 | tf_op jit(solution)/shard_map/ppermute | solution.py:558
  86.8 0.0 collective-permute-done.13.refs_2_
  86.8 0.9 collective-permute-done.14.refs_3_
  87.7 0.0 copy-start.3
  87.7 10.2 %backward_attention.1 = f32[32,512]{1,0:T(8,128)S(1)} custom-call(s32[1]{0:T(128)} %bitcast.2.y_ref, bf16[32,512]{1,0:T(8,128)(2,1)S(1)} %get-tuple-element.49.refs_1_.refs_2_.q_ref, bf16[4,8,640]{2,1,0:T(8,128)(2,1)S(1)} %bitcast.27, bf16[4,8,640]{2,1,0:T(8,128)(2,1)S(1)} %collective-permute-done.12.refs_1_, ...), custom_call_target="tpu_custom_call" | custom-call | tf_op jit(solution)/shard_map/backward_attention/pallas_call | solution.py:486
  97.9 0.1 copy.20
  98.0 14.5 %all_to_all.19 = f32[32,1,512]{2,1,0:T(1,128)S(1)} all-to-all(f32[32,1,512]{2,1,0:T(1,128)S(1)} %copy.20), channel_id=1, replica_groups=mesh['y'=4,'z'=8,'tm'=8] {'y','tm'}, dimensions={0} | all-to-all | bytes 131072 | tf_op jit(solution)/shard_map/all_to_all | solution.py:561
  112.4 0.1 reduce_sum.9
  112.5 0.1 broadcast_in_dim.2
  112.6 23.9 %all_to_all.20 = bf16[256,4,128]{2,1,0:T(4,128)(2,1)S(1)} all-to-all(bf16[256,4,128]{2,1,0:T(4,128)(2,1)S(1)} %broadcast_in_dim.2), channel_id=1, replica_groups=mesh['y'=4,'z'=8,'tm'=8] {'y','z','tm'}, dimensions={0} | all-to-all | bytes 524288 | tf_op jit(solution)/shard_map/all_to_all | solution.py:564
  136.5 0.0 copy-done.3
  136.5 1.1 fusion
  (1 shorter events, 0.0 us)
Async XLA Ops:
  2.2 13.1 %collective-permute-start = (bf16[256,256]{1,0:T(8,128)(2,1)S(1)}, bf16[256,256]{1,0:T(8,128)(2,1)S(1)}, u32[]{:S(2)}, u32[]{:S(2)}) collective-permute-start(bf16[256,256]{1,0:T(8,128)(2,1)S(1)} %make_message.1.refs_0_), channel_id=1, source_target_pairs={{0,8},{8,16},{16,24},{24,32},{32,40},{40,48},{48,56},{56,0},{1,9},... | collective-permute-start | bytes 393224 | tf_op jit(solution)/shard_map/ppermute | solution.py:529
  4.7 10.6 %collective-permute-start.1 = (bf16[256,256]{1,0:T(8,128)(2,1)S(1)}, bf16[256,256]{1,0:T(8,128)(2,1)S(1)}, u32[]{:S(2)}, u32[]{:S(2)}) collective-permute-start(bf16[256,256]{1,0:T(8,128)(2,1)S(1)} %make_message.1.refs_0_), channel_id=1, source_target_pairs={{0,56},{8,0},{16,8},{24,16},{32,24},{40,32},{48,40},{56,48},{1,57}... | collective-permute-start | bytes 393224 | tf_op jit(solution)/shard_map/ppermute | solution.py:531
  15.3 11.2 %collective-permute-start.2 = (bf16[256,256]{1,0:T(8,128)(2,1)S(1)}, bf16[256,256]{1,0:T(8,128)(2,1)S(1)}, u32[]{:S(2)}, u32[]{:S(2)}) collective-permute-start(bf16[256,256]{1,0:T(8,128)(2,1)S(1)} %collective-permute-done.refs_0_), channel_id=1, source_target_pairs={{0,8},{8,16},{16,24},{24,32},{32,40},{40,48},{48,56},{56,0},{1,9},... | collective-permute-start | bytes 393224 | tf_op jit(solution)/shard_map/ppermute | solution.py:529
  15.4 11.1 %collective-permute-start.3 = (bf16[256,256]{1,0:T(8,128)(2,1)S(1)}, bf16[256,256]{1,0:T(8,128)(2,1)S(1)}, u32[]{:S(2)}, u32[]{:S(2)}) collective-permute-start(bf16[256,256]{1,0:T(8,128)(2,1)S(1)} %collective-permute-done.1.refs_1_), channel_id=1, source_target_pairs={{0,56},{8,0},{16,8},{24,16},{32,24},{40,32},{48,40},{56,48},{1,57}... | collective-permute-start | bytes 393224 | tf_op jit(solution)/shard_map/ppermute | solution.py:531
  26.5 11.2 %collective-permute-start.4 = (bf16[256,256]{1,0:T(8,128)(2,1)S(1)}, bf16[256,256]{1,0:T(8,128)(2,1)S(1)}, u32[]{:S(2)}, u32[]{:S(2)}) collective-permute-start(bf16[256,256]{1,0:T(8,128)(2,1)S(1)} %collective-permute-done.2.refs_0_), channel_id=1, source_target_pairs={{0,8},{8,16},{16,24},{24,32},{32,40},{40,48},{48,56},{56,0},{1,9},... | collective-permute-start | bytes 393224 | tf_op jit(solution)/shard_map/ppermute | solution.py:529
  26.6 11.1 %collective-permute-start.5 = (bf16[256,256]{1,0:T(8,128)(2,1)S(1)}, bf16[256,256]{1,0:T(8,128)(2,1)S(1)}, u32[]{:S(2)}, u32[]{:S(2)}) collective-permute-start(bf16[256,256]{1,0:T(8,128)(2,1)S(1)} %collective-permute-done.3.refs_1_), channel_id=1, source_target_pairs={{0,56},{8,0},{16,8},{24,16},{32,24},{40,32},{48,40},{56,48},{1,57}... | collective-permute-start | bytes 393224 | tf_op jit(solution)/shard_map/ppermute | solution.py:531
  37.7 8.5 %collective-permute-start.6 = (bf16[256,256]{1,0:T(8,128)(2,1)S(1)}, bf16[256,256]{1,0:T(8,128)(2,1)S(1)}, u32[]{:S(2)}, u32[]{:S(2)}) collective-permute-start(bf16[256,256]{1,0:T(8,128)(2,1)S(1)} %collective-permute-done.4.refs_0_), channel_id=1, source_target_pairs={{0,8},{8,16},{16,24},{24,32},{32,40},{40,48},{48,56},{56,0},{1,9},... | collective-permute-start | bytes 393224 | tf_op jit(solution)/shard_map/ppermute | solution.py:529
  46.3 22.2 %copy-start.1 = (bf16[4,8,512]{2,1,0:T(8,128)(2,1)S(1)}, bf16[4,8,512]{2,1,0:T(8,128)(2,1)}, u32[]{:S(2)}) copy-start(bf16[4,8,512]{2,1,0:T(8,128)(2,1)} %param.23) | copy-start | bytes 98308
  46.3 30.9 %copy-start = (bf16[512,512]{1,0:T(8,128)(2,1)S(1)}, bf16[512,512]{1,0:T(8,128)(2,1)}, u32[]{:S(2)}) copy-start(bf16[512,512]{1,0:T(8,128)(2,1)} %w_out_ref.1) | copy-start | bytes 1572868
  46.3 30.9 %copy-start.2 = (f32[2,512]{1,0:T(2,128)S(1)}, f32[2,512]{1,0:T(2,128)}, u32[]{:S(2)}) copy-start(f32[2,512]{1,0:T(2,128)} %bias_ref.1) | copy-start | bytes 12292
  50.9 4.5 %collective-permute-start.7 = (f32[4,8,640]{2,1,0:T(8,128)S(1)}, f32[4,8,640]{2,1,0:T(8,128)S(1)}, u32[]{:S(2)}, u32[]{:S(2)}) collective-permute-start(f32[4,8,640]{2,1,0:T(8,128)S(1)} %get-tuple-element.71), channel_id=1, source_target_pairs={{0,192},{64,0},{128,64},{192,128},{1,193},{65,1},{129,65},{193,129... | collective-permute-start | bytes 245768 | tf_op jit(solution)/shard_map/ppermute | solution.py:542
  53.9 4.9 %collective-permute-start.8 = (f32[4,8,640]{2,1,0:T(8,128)S(1)}, f32[4,8,640]{2,1,0:T(8,128)S(1)}, u32[]{:S(2)}, u32[]{:S(2)}) collective-permute-start(f32[4,8,640]{2,1,0:T(8,128)S(1)} %get-tuple-element.72), channel_id=1, source_target_pairs={{0,128},{64,192},{128,0},{192,64},{1,129},{65,193},{129,1},{193,65... | collective-permute-start | bytes 245768 | tf_op jit(solution)/shard_map/ppermute | solution.py:542
  54.3 5.3 %collective-permute-start.9 = (f32[4,8,640]{2,1,0:T(8,128)S(1)}, f32[4,8,640]{2,1,0:T(8,128)S(1)}, u32[]{:S(2)}, u32[]{:S(2)}) collective-permute-start(f32[4,8,640]{2,1,0:T(8,128)S(1)} %get-tuple-element.73), channel_id=1, source_target_pairs={{0,64},{64,128},{128,192},{192,0},{1,65},{65,129},{129,193},{193,1... | collective-permute-start | bytes 245768 | tf_op jit(solution)/shard_map/ppermute | solution.py:542
  60.7 16.5 %all-to-all-start = ((bf16[8,32,512]{2,1,0:T(8,128)(2,1)}), bf16[8,32,512]{2,1,0:T(8,128)(2,1)S(1)}, u32[]{:S(2)}, u32[]{:S(2)}) async-start(bf16[8,32,512]{2,1,0:T(8,128)(2,1)} %get-tuple-element.75), calls=%async_computation | async-start | bytes 524288 | tf_op jit(solution)/shard_map/all_to_all | solution.py:551
  68.5 5.5 %collective-permute-start.10 = (bf16[24,512]{1,0:T(8,128)(2,1)S(1)}, bf16[24,512]{1,0:T(8,128)(2,1)S(1)}, u32[]{:S(2)}, u32[]{:S(2)}) collective-permute-start(bf16[24,512]{1,0:T(8,128)(2,1)S(1)} %get-tuple-element.77), channel_id=1, source_target_pairs={{0,1},{1,2},{2,3},{3,4},{4,5},{5,6},{6,7},{8,9},{9,10},{10,11},{11... | collective-permute-start | bytes 73736 | tf_op jit(solution)/shard_map/ppermute | solution.py:546
  72.1 5.1 %collective-permute-start.11 = (bf16[24,512]{1,0:T(8,128)(2,1)S(1)}, bf16[24,512]{1,0:T(8,128)(2,1)S(1)}, u32[]{:S(2)}, u32[]{:S(2)}) collective-permute-start(bf16[24,512]{1,0:T(8,128)(2,1)S(1)} %get-tuple-element.78), channel_id=1, source_target_pairs={{1,0},{2,1},{3,2},{4,3},{5,4},{6,5},{7,6},{9,8},{10,9},{11,10},{12... | collective-permute-start | bytes 73736 | tf_op jit(solution)/shard_map/ppermute | solution.py:547
  82.1 4.7 %collective-permute-start.12 = (bf16[4,8,640]{2,1,0:T(8,128)(2,1)S(1)}, bf16[4,8,640]{2,1,0:T(8,128)(2,1)S(1)}, u32[]{:S(2)}, u32[]{:S(2)}) collective-permute-start(bf16[4,8,640]{2,1,0:T(8,128)(2,1)S(1)} %bitcast.24), channel_id=1, source_target_pairs={{0,64},{64,128},{128,192},{192,0},{1,65},{65,129},{129,193},{193,1... | collective-permute-start | bytes 122888 | tf_op jit(solution)/shard_map/ppermute | solution.py:558
  82.2 4.6 %collective-permute-start.13 = (bf16[4,8,640]{2,1,0:T(8,128)(2,1)S(1)}, bf16[4,8,640]{2,1,0:T(8,128)(2,1)S(1)}, u32[]{:S(2)}, u32[]{:S(2)}) collective-permute-start(bf16[4,8,640]{2,1,0:T(8,128)(2,1)S(1)} %bitcast.25), channel_id=1, source_target_pairs={{0,128},{64,192},{128,0},{192,64},{1,129},{65,193},{129,1},{193,65... | collective-permute-start | bytes 122888 | tf_op jit(solution)/shard_map/ppermute | solution.py:558
  83.6 4.0 %collective-permute-start.14 = (bf16[4,8,640]{2,1,0:T(8,128)(2,1)S(1)}, bf16[4,8,640]{2,1,0:T(8,128)(2,1)S(1)}, u32[]{:S(2)}, u32[]{:S(2)}) collective-permute-start(bf16[4,8,640]{2,1,0:T(8,128)(2,1)S(1)} %bitcast.26), channel_id=1, source_target_pairs={{0,192},{64,0},{128,64},{192,128},{1,193},{65,1},{129,65},{193,129... | collective-permute-start | bytes 122888 | tf_op jit(solution)/shard_map/ppermute | solution.py:558
  87.7 48.9 %copy-start.3 = (bf16[512,512]{1,0:T(8,128)(2,1)S(1)}, bf16[512,512]{1,0:T(8,128)(2,1)}, u32[]{:S(2)}) copy-start(bf16[512,512]{1,0:T(8,128)(2,1)} %refs_4_.1) | copy-start | bytes 1572868
